TPU v7x, 32 devices: a whole 2x2x4 slice. The times are simulated.
32 devices in a mesh: dp: 8 (over z, y), ns: 4 (over x, core).
Axes of the slice: x: 2, y: 2, z: 4, core: 2. Of those that a mesh axis runs over, the one named last changes fastest.
Arguments:
- patches: bfloat16 [32768, 768], P(('dp', 'ns')), may hold values from -6 to 6
- masked: int32 [32768], P(('dp', 'ns')), may hold values from 0 to 1, as said below
- counts: int32 [32], P(('dp', 'ns')), may hold values from 64 to 1024, as said below
- hog_targets: bfloat16 [108, 32768], P(None, ('dp', 'ns')), may hold values from -6 to 6
- qkv_weight: float32 [768, 2304], P(None, ('dp', 'ns')), may hold values from -0.3125 to 0.3125
- out_weight: float32 [768, 768], P(('dp', 'ns')), may hold values from -1.25 to 1.25
- fc1_weight: float32 [768, 3072], P(None, ('dp', 'ns')), may hold values from -0.21875 to 0.21875
- fc2_weight: float32 [3072, 768], P(('dp', 'ns')), may hold values from -0.109375 to 0.109375
- head_weight: float32 [768, 108], P(('dp', 'ns')), may hold values from -0.21875 to 0.21875
- vectors: float32 [13, 768], P(None, ('dp', 'ns')), may hold values from -4 to 4
- qkv_moment: float32 [768, 2304], P(None, ('dp', 'ns')), may hold values from -0.001953125 to 0.001953125
- out_moment: float32 [768, 768], P(('dp', 'ns')), may hold values from -0.001953125 to 0.001953125
- fc1_moment: float32 [768, 3072], P(None, ('dp', 'ns')), may hold values from -0.001953125 to 0.001953125
- fc2_moment: float32 [3072, 768], P(('dp', 'ns')), may hold values from -0.001953125 to 0.001953125
- head_first: float32 [768, 108], P(('dp', 'ns')), may hold values from -0.00024414062 to 0.00024414062
- head_second: float32 [768, 108], P(('dp', 'ns')), may hold values from 8.3789145e-09 to 3.072269e-08
- vector_first: float32 [13, 768], P(None, ('dp', 'ns')), may hold values from -0.0007324219 to 0.0007324219
- vector_second: float32 [13, 768], P(None, ('dp', 'ns')), may hold values from 6.982429e-08 to 2.7929715e-07
Outputs:
- block_output: bfloat16 [32768, 768], P(('dp', 'ns'))
- patch_grads: float32 [32768, 768], P(('dp', 'ns'))
- grad_norm: float32 [], replicated
- qkv_moment_new: float32 [768, 2304], P(None, ('dp', 'ns'))
- out_moment_new: float32 [768, 768], P(('dp', 'ns'))
- fc1_moment_new: float32 [768, 3072], P(None, ('dp', 'ns'))
- fc2_moment_new: float32 [3072, 768], P(('dp', 'ns'))
- qkv_new: float32 [768, 2304], P(None, ('dp', 'ns'))
- out_new: float32 [768, 768], P(('dp', 'ns'))
- fc1_new: float32 [768, 3072], P(None, ('dp', 'ns'))
- fc2_new: float32 [3072, 768], P(('dp', 'ns'))
- qkv_copy: bfloat16 [768, 2304], P(None, ('dp', 'ns'))
- out_copy: bfloat16 [768, 768], P(('dp', 'ns'))
- fc1_copy: bfloat16 [768, 3072], P(None, ('dp', 'ns'))
- fc2_copy: bfloat16 [3072, 768], P(('dp', 'ns'))
- head_first_new: float32 [768, 108], P(('dp', 'ns'))
- head_second_new: float32 [768, 108], P(('dp', 'ns'))
- head_new: float32 [768, 108], P(('dp', 'ns'))
- head_copy: bfloat16 [768, 108], P(('dp', 'ns'))
- vector_first_new: float32 [13, 768], P(None, ('dp', 'ns'))
- vector_second_new: float32 [13, 768], P(None, ('dp', 'ns'))
- vectors_new: float32 [13, 768], P(None, ('dp', 'ns'))
- vectors_copy: bfloat16 [13, 768], P(None, ('dp', 'ns'))
Inputs may be any that keep to these rules, and one draw needn't show every extreme that they name: The first slot of every image is masked. `counts`: an image's valid patches are its first slots; in every draw some image has all 1024 slots valid.
All inputs are finite; a program needn't handle non-finite values.
Results may differ from a plain program's by a relative error of at most 0.006.
The roundings to bfloat16 on the way count: a program that leaves them out, or rounds other values in their place, can miss the bound.
Values may be sent and summed in bfloat16 or wider, within the bound.
A program may use at most 320 MiB of HBM per device.

v0:
```python
from functools import partial
import math

import jax
import jax.numpy as jnp
from jax import lax
from jax.sharding import PartitionSpec as P

HEADS = 12
HEAD_DIM = 64


newton_first = 3.4445
newton_second = -4.775
newton_third = 2.0315
muon_rate = 0.5
muon_decay = 0.01
momentum_keep = 0.5
beta_first = 0.9
beta_second = 0.95
head_rate = 0.1
head_decay = 0.01
vector_rate = 0.3
highest = lax.Precision.HIGHEST


def norm_forward(row_data):
    center = row_data - jnp.mean(row_data, axis=-1, keepdims=True)
    spread = jnp.mean(center * center, axis=-1, keepdims=True)
    inverse = lax.rsqrt(spread + 1e-06)
    return (center * inverse, inverse)


def norm_backward(grad_rows, normed, inverse, gain):
    scaled = grad_rows * gain
    first_mean = jnp.mean(scaled, axis=-1, keepdims=True)
    second_mean = jnp.mean(scaled * normed, axis=-1, keepdims=True)
    return inverse * (scaled - first_mean - normed * second_mean)


def score_block(queries, key_rows, live_mask):
    scores = (
        jnp.einsum("qhe,khe->hqk", queries, key_rows, preferred_element_type=jnp.float32) * 0.125
    )
    return jnp.where(live_mask[None, None, :], scores, -1e30)


def attend_span(queries, key_rows, value_rows, live_mask):
    scores = score_block(queries, key_rows, live_mask)
    summit = jnp.max(scores, axis=-1, keepdims=True)
    raised = jnp.exp(scores - summit)
    denominator = jnp.sum(raised, axis=-1, keepdims=True)
    attn_weights = (raised / denominator).astype(jnp.bfloat16)
    mixture = jnp.einsum(
        "hqk,khe->qhe", attn_weights, value_rows, preferred_element_type=jnp.float32
    )
    return (mixture, (summit + jnp.log(denominator))[..., 0])


def attend_back_span(queries, key_rows, value_rows, live_mask, log_total, grad_mix):
    scores = score_block(queries, key_rows, live_mask)
    attn_weights = jnp.exp(scores - log_total[..., None])
    grad_weights = jnp.einsum(
        "qhe,khe->hqk", grad_mix, value_rows, preferred_element_type=jnp.float32
    )
    inner_sum = jnp.sum(attn_weights * grad_weights, axis=-1, keepdims=True)
    grad_scores = (attn_weights * (grad_weights - inner_sum)).astype(jnp.bfloat16)
    grad_queries = (
        jnp.einsum("hqk,khe->qhe", grad_scores, key_rows, preferred_element_type=jnp.float32)
        * 0.125
    )
    grad_keys = (
        jnp.einsum("hqk,qhe->khe", grad_scores, queries, preferred_element_type=jnp.float32) * 0.125
    )
    grad_values = jnp.einsum(
        "hqk,qhe->khe",
        attn_weights.astype(jnp.bfloat16),
        grad_mix,
        preferred_element_type=jnp.float32,
    )
    return (grad_queries, grad_keys, grad_values)


def newton_steps(stacked, gram_total):
    for newton_turn in range(5):
        gram_local = jnp.einsum("mrd,mre->mde", stacked, stacked, precision=highest)
        gram_matrix = gram_total(gram_local)
        first_term = jnp.einsum("mrd,mde->mre", stacked, gram_matrix, precision=highest)
        second_term = jnp.einsum("mrd,mde->mre", first_term, gram_matrix, precision=highest)
        stacked = newton_first * stacked + newton_second * first_term + newton_third * second_term
    return stacked


def adam_update(weight, first_old, second_old, grad_piece, rate, decay):
    first_new = beta_first * first_old + (1.0 - beta_first) * grad_piece
    second_new = beta_second * second_old + (1.0 - beta_second) * grad_piece * grad_piece
    weight_new = weight - rate * (first_new / (jnp.sqrt(second_new) + 1e-08) + decay * weight)
    return (first_new, second_new, weight_new)


def local(
    patches,
    masked,
    counts,
    hog_targets,
    qkv_weight,
    out_weight,
    fc1_weight,
    fc2_weight,
    head_weight,
    vectors,
    qkv_moment,
    out_moment,
    fc1_moment,
    fc2_moment,
    head_first,
    head_second,
    vector_first,
    vector_second,
):
    half_type = jnp.bfloat16
    qkv_full, fc1_full, vector_low = (
        lax.all_gather(qkv_weight.astype(half_type), ("dp", "ns"), axis=1, tiled=True),
        lax.all_gather(fc1_weight.astype(half_type), ("dp", "ns"), axis=1, tiled=True),
        lax.all_gather(vectors.astype(half_type), ("dp", "ns"), axis=1, tiled=True),
    )
    out_full, fc2_full, head_full = (
        lax.all_gather(out_weight.astype(half_type), ("dp", "ns"), axis=0, tiled=True),
        lax.all_gather(fc2_weight.astype(half_type), ("dp", "ns"), axis=0, tiled=True),
        lax.all_gather(head_weight.astype(half_type), ("dp", "ns"), axis=0, tiled=True),
    )
    vector_rows = vector_low.astype(jnp.float32)
    model_width = out_full.shape[1]
    hidden_units = fc1_full.shape[1]
    image_count = counts.shape[0]
    row_count = patches.shape[0]
    seq_len = row_count // image_count
    block_rows = min(512, seq_len)
    slot_place = jnp.arange(seq_len)
    live_rows = (slot_place[None, :] < counts[:, None]).reshape(row_count)
    masked_here = masked == 1
    chosen = (
        jnp.logical_and(masked_here, live_rows).astype(jnp.float32).reshape(image_count, seq_len)
    )
    loss_weight = (chosen / jnp.sum(chosen, axis=1, keepdims=True)).reshape(row_count)
    stream = jnp.where(masked_here[:, None], vector_rows[8][None, :], patches.astype(jnp.float32))
    normed_one, inverse_one = norm_forward(stream)
    input_one = (normed_one * vector_rows[0] + vector_rows[1]).astype(half_type)
    qkv_bias = jnp.concatenate([vector_rows[2], jnp.zeros_like(vector_rows[2]), vector_rows[3]])
    joined = (jnp.dot(input_one, qkv_full, preferred_element_type=jnp.float32) + qkv_bias).astype(
        half_type
    )
    heads_shape = (row_count, HEADS, HEAD_DIM)
    queries = joined[:, :model_width].reshape(heads_shape)
    key_rows = joined[:, model_width : 2 * model_width].reshape(heads_shape)
    value_rows = joined[:, 2 * model_width :].reshape(heads_shape)
    mix_parts = []
    log_parts = []
    image_index = 0
    first_row = image_index * seq_len
    live_mask = slot_place < counts[image_index]
    for block_start in range(first_row, first_row + seq_len, block_rows):
        block_queries = queries[block_start : block_start + block_rows]
        block_result = attend_span(block_queries, key_rows, value_rows, live_mask)
        mix_parts.append(block_result[0])
        log_parts.append(block_result[1])
    mixture = jnp.concatenate(mix_parts, axis=0).reshape(row_count, model_width).astype(half_type)
    after_attn = stream + (
        jnp.dot(mixture, out_full, preferred_element_type=jnp.float32) + vector_rows[4]
    )
    normed_two, inverse_two = norm_forward(after_attn)
    input_two = (normed_two * vector_rows[5] + vector_rows[6]).astype(half_type)
    pre_act = jnp.dot(input_two, fc1_full, preferred_element_type=jnp.float32) + vector_rows[
        9:
    ].reshape(hidden_units)
    activation, gelu_back = jax.vjp(partial(jax.nn.gelu, approximate=False), pre_act)
    act_low = activation.astype(half_type)
    after_mlp = after_attn + (
        jnp.dot(act_low, fc2_full, preferred_element_type=jnp.float32) + vector_rows[7]
    )
    hidden = after_mlp.astype(half_type)
    predicted = jnp.einsum("dh,td->ht", head_full, hidden, preferred_element_type=jnp.float32)
    misfit = predicted - hog_targets.astype(jnp.float32)
    grad_pred = (2.0 * misfit * loss_weight[None, :]).astype(half_type)
    grad_head = jnp.einsum("td,ht->dh", hidden, grad_pred, preferred_element_type=jnp.float32)
    grad_stream = jnp.einsum("ht,dh->td", grad_pred, head_full, preferred_element_type=jnp.float32)
    grad_branch = grad_stream.astype(half_type)
    grad_fc2 = jnp.einsum("tf,td->fd", act_low, grad_branch, preferred_element_type=jnp.float32)
    grad_fc2_bias = jnp.sum(grad_branch.astype(jnp.float32), axis=0)
    grad_act = jnp.einsum("td,fd->tf", grad_branch, fc2_full, preferred_element_type=jnp.float32)
    grad_pre = gelu_back(grad_act)[0].astype(half_type)
    grad_fc1 = jnp.einsum("td,tf->df", input_two, grad_pre, preferred_element_type=jnp.float32)
    grad_fc1_bias = jnp.sum(grad_pre.astype(jnp.float32), axis=0)
    grad_two = jnp.einsum("tf,df->td", grad_pre, fc1_full, preferred_element_type=jnp.float32)
    grad_gain_two = jnp.sum(grad_two * normed_two, axis=0)
    grad_shift_two = jnp.sum(grad_two, axis=0)
    grad_stream = grad_stream + norm_backward(grad_two, normed_two, inverse_two, vector_rows[5])
    grad_attn = grad_stream.astype(half_type)
    grad_out = jnp.einsum("te,td->ed", mixture, grad_attn, preferred_element_type=jnp.float32)
    grad_out_bias = jnp.sum(grad_attn.astype(jnp.float32), axis=0)
    grad_mix = (
        jnp.einsum("td,ed->te", grad_attn, out_full, preferred_element_type=jnp.float32)
        .astype(half_type)
        .reshape(heads_shape)
    )
    query_parts = []
    image_index = 0
    first_row = image_index * seq_len
    live_mask = slot_place < counts[image_index]
    key_total = jnp.zeros((seq_len, HEADS, HEAD_DIM), jnp.float32)
    value_total = jnp.zeros((seq_len, HEADS, HEAD_DIM), jnp.float32)
    for block_start in range(first_row, first_row + seq_len, block_rows):
        block_queries = queries[block_start : block_start + block_rows]
        block_grad = grad_mix[block_start : block_start + block_rows]
        log_total = log_parts[block_start // block_rows]
        pieces = attend_back_span(
            block_queries, key_rows, value_rows, live_mask, log_total, block_grad
        )
        query_parts.append(pieces[0])
        key_total = key_total + pieces[1]
        value_total = value_total + pieces[2]
    grad_joined = jnp.concatenate(
        [
            jnp.concatenate(query_parts, axis=0).reshape(row_count, model_width),
            key_total.reshape(row_count, model_width),
            value_total.reshape(row_count, model_width),
        ],
        axis=1,
    ).astype(half_type)
    grad_qkv = jnp.einsum("td,te->de", input_one, grad_joined, preferred_element_type=jnp.float32)
    grad_query_bias = jnp.sum(grad_joined[:, :model_width].astype(jnp.float32), axis=0)
    grad_value_bias = jnp.sum(grad_joined[:, 2 * model_width :].astype(jnp.float32), axis=0)
    grad_one = jnp.einsum("te,de->td", grad_joined, qkv_full, preferred_element_type=jnp.float32)
    grad_gain_one = jnp.sum(grad_one * normed_one, axis=0)
    grad_shift_one = jnp.sum(grad_one, axis=0)
    grad_stream = grad_stream + norm_backward(grad_one, normed_one, inverse_one, vector_rows[0])
    grad_token = jnp.sum(jnp.where(masked_here[:, None], grad_stream, 0.0), axis=0)
    patch_grads = jnp.where(masked_here[:, None], 0.0, grad_stream)
    grad_vectors = jnp.concatenate(
        [
            jnp.stack(
                [
                    grad_gain_one,
                    grad_shift_one,
                    grad_query_bias,
                    grad_value_bias,
                    grad_out_bias,
                    grad_gain_two,
                    grad_shift_two,
                    grad_fc2_bias,
                    grad_token,
                ]
            ),
            grad_fc1_bias.reshape(-1, model_width),
        ],
        axis=0,
    )
    qkv_grad, fc1_grad, vector_grad = (
        lax.psum_scatter(grad_qkv, ("dp", "ns"), scatter_dimension=1, tiled=True),
        lax.psum_scatter(grad_fc1, ("dp", "ns"), scatter_dimension=1, tiled=True),
        lax.psum_scatter(grad_vectors, ("dp", "ns"), scatter_dimension=1, tiled=True),
    )
    out_grad, fc2_grad, head_grad = (
        lax.psum_scatter(grad_out, ("dp", "ns"), scatter_dimension=0, tiled=True),
        lax.psum_scatter(grad_fc2, ("dp", "ns"), scatter_dimension=0, tiled=True),
        lax.psum_scatter(grad_head, ("dp", "ns"), scatter_dimension=0, tiled=True),
    )
    every_grad = (qkv_grad, out_grad, fc1_grad, fc2_grad, head_grad, vector_grad)
    square_sum = jnp.sum(jnp.stack([jnp.sum(grad_piece * grad_piece) for grad_piece in every_grad]))
    old_moments = (qkv_moment, out_moment, fc1_moment, fc2_moment)
    muon_grads = (qkv_grad, out_grad, fc1_grad, fc2_grad)
    square_total = lax.psum(square_sum, ("dp", "ns"))
    grad_norm = jnp.sqrt(square_total)
    shrink = jnp.minimum(1.0, 1.0 / (grad_norm + 1e-06))
    new_moments = tuple(
        (
            momentum_keep * old_mom + shrink * grad_piece
            for old_mom, grad_piece in zip(old_moments, muon_grads)
        )
    )
    moment_norms = jnp.sqrt(
        lax.psum(jnp.stack([jnp.sum(new_mom * new_mom) for new_mom in new_moments]), ("dp", "ns"))
    )
    tall_forms = (new_moments[0].T, new_moments[1], new_moments[2].T, new_moments[3])
    tall_rows = max((tall_piece.shape[0] for tall_piece in tall_forms))
    stacked = jnp.stack(
        [
            jnp.pad(
                tall_piece / (moment_norms[slot_index] + 1e-07),
                ((0, tall_rows - tall_piece.shape[0]), (0, 0)),
            )
            for slot_index, tall_piece in enumerate(tall_forms)
        ]
    )

    def spread_total(gram_local):
        gram_rows = lax.psum_scatter(gram_local, ("dp", "ns"), scatter_dimension=1, tiled=True)
        return lax.all_gather(gram_rows, ("dp", "ns"), axis=1, tiled=True)

    finished = newton_steps(stacked, spread_total)
    long_sizes = (qkv_full.shape[1], model_width, hidden_units, hidden_units)
    old_weights = (qkv_weight, out_weight, fc1_weight, fc2_weight)
    updates = (
        finished[0, : qkv_weight.shape[1]].T,
        finished[1, : out_weight.shape[0]],
        finished[2, : fc1_weight.shape[1]].T,
        finished[3, : fc2_weight.shape[0]],
    )
    new_weights = tuple(
        (
            old_weight
            - muon_rate
            * (
                math.sqrt(max(1.0, long_size / model_width)) * update_piece
                + muon_decay * old_weight
            )
            for old_weight, update_piece, long_size in zip(old_weights, updates, long_sizes)
        )
    )
    head_first_new, head_second_new, head_new = adam_update(
        head_weight, head_first, head_second, shrink * head_grad, head_rate, head_decay
    )
    vector_first_new, vector_second_new, vectors_new = adam_update(
        vectors, vector_first, vector_second, shrink * vector_grad, vector_rate, 0.0
    )
    return (
        hidden,
        patch_grads,
        grad_norm,
        new_moments[0],
        new_moments[1],
        new_moments[2],
        new_moments[3],
        new_weights[0],
        new_weights[1],
        new_weights[2],
        new_weights[3],
        new_weights[0].astype(half_type),
        new_weights[1].astype(half_type),
        new_weights[2].astype(half_type),
        new_weights[3].astype(half_type),
        head_first_new,
        head_second_new,
        head_new,
        head_new.astype(half_type),
        vector_first_new,
        vector_second_new,
        vectors_new,
        vectors_new.astype(half_type),
    )


def solution(mesh):
    placed = (
        P(("dp", "ns"), None),
        P(("dp", "ns")),
        P(("dp", "ns")),
        P(None, ("dp", "ns")),
        P(None, ("dp", "ns")),
        P(("dp", "ns"), None),
        P(None, ("dp", "ns")),
        P(("dp", "ns"), None),
        P(("dp", "ns"), None),
        P(None, ("dp", "ns")),
        P(None, ("dp", "ns")),
        P(("dp", "ns"), None),
        P(None, ("dp", "ns")),
        P(("dp", "ns"), None),
        P(("dp", "ns"), None),
        P(("dp", "ns"), None),
        P(None, ("dp", "ns")),
        P(None, ("dp", "ns")),
    )
    return jax.shard_map(
        local,
        mesh=mesh,
        in_specs=placed,
        out_specs=(
            P(("dp", "ns"), None),
            P(("dp", "ns"), None),
            P(),
            P(None, ("dp", "ns")),
            P(("dp", "ns"), None),
            P(None, ("dp", "ns")),
            P(("dp", "ns"), None),
            P(None, ("dp", "ns")),
            P(("dp", "ns"), None),
            P(None, ("dp", "ns")),
            P(("dp", "ns"), None),
            P(None, ("dp", "ns")),
            P(("dp", "ns"), None),
            P(None, ("dp", "ns")),
            P(("dp", "ns"), None),
            P(("dp", "ns"), None),
            P(("dp", "ns"), None),
            P(("dp", "ns"), None),
            P(("dp", "ns"), None),
            P(None, ("dp", "ns")),
            P(None, ("dp", "ns")),
            P(None, ("dp", "ns")),
            P(None, ("dp", "ns")),
        ),
        check_vma=False,
    )
```

profile of v0, /device:TPU:1, one launch (start us, length us, event | category | flops | bytes accessed | tf_op | source)
XLA Modules:
  0.0 2267.2 jit_solution(13624435919130799767)
XLA Ops:
  14.7 43.6 %all-gather = bf16[32,24,13]{1,2,0:T(8,128)(2,1)S(1)} all-gather(bf16[1,24,13]{1,2,0:T(8,128)(2,1)S(1)} %convert_bitcast_fusion), channel_id=1, replica_groups=mesh['dp'=8,'ns'=4] {'dp','ns'}, dimensions={0}, use_global_device_ids=true | all-gather | bytes 20592 | tf_op jit(solution)/shard_map/all_gather | solution.py:125
  63.6 40.0 %all_gather.38 = bf16[768,108]{1,0:T(8,128)(2,1)} all-gather(bf16[24,108]{1,0:T(8,128)(2,1)S(1)} %convert_element_type.135), channel_id=1, replica_groups=mesh['dp'=8,'ns'=4] {'dp','ns'}, dimensions={0}, use_global_device_ids=true | all-gather | bytes 171072 | tf_op jit(solution)/shard_map/all_gather | solution.py:130
  122.4 12.2 fusion.18
  134.6 20.7 fusion
  155.3 11.2 fusion.1
  166.5 11.2 fusion.36
  177.7 11.4 fusion.37
  197.0 36.9 %multiply_convert_fusion.2 = (bf16[1024,3072]{1,0:T(8,128)(2,1)}, f32[1024,3072]{1,0:T(8,128)}, f32[1024,3072]{1,0:T(8,128)}) fusion(f32[3072]{0:T(1024)S(1)} %add.270, bf16[768,3072]{0,1:T(8,128)(2,1)} %all-gather.15.cloned.1.call-done, f32[1024,768]{1,0:T(8,128)} %copy-done.13, f32[768]{0:T(1024)S(1)} %get-tuple-element.32, ...), kind=kOutput, calls=%fused_computation.24 | convolution fusion | flops 5043388416 | bytes 39348224 | tf_op jit(solution)/shard_map/dot_general | solution.py:173
  233.9 28.8 %all-gather.17.cloned.1.call-done = bf16[3072,768]{1,0:T(8,128)(2,1)} async-done(((bf16[96,768]{1,0:T(8,128)(2,1)}), bf16[3072,768]{1,0:T(8,128)(2,1)}) %all-gather.17.cloned.1.call-update) | async-done | bytes 4718608 | tf_op jit(solution)/shard_map/all_gather | solution.py:129
  277.2 19.6 convert_reduce_fusion
  322.4 13.1 fusion.5
  335.5 35.4 %multiply_reduce_fusion = (f32[12,512]{1,0:T(8,128)S(1)}, f32[12,512]{1,0:T(8,128)S(1)}, f32[12,512,1024]{2,1,0:T(8,128)}) fusion(f32[12,512]{1,0:T(8,128)S(1)} %copy-done.41, f32[12,512,1024]{2,1,0:T(8,128)} %get-tuple-element.91, pred[1024]{0:T(1024)(128)(4,1)S(1)} %copy-done.63, f32[12,512,1024]{2,1,0:T(8,128)} %fusion.100, f32[12,512]{1,0:T(8,128)S(1)} %copy-done.40, ...), kind=kOutput, calls=%fused_computation.1 | convolution fusion | flops 868208640 | bytes 103121920 | tf_op jit(solution)/shard_map/qhe,khe->hqk/dot_general | solution.py:63
  370.9 41.6 %multiply_convert_fusion = (bf16[12,512,1024]{2,1,0:T(8,128)(2,1)}, bf16[12,512,1024]{2,1,0:T(8,128)(2,1)}) fusion(f32[12,512,1024]{2,1,0:T(8,128)} %get-tuple-element.96, f32[12,512]{1,0:T(8,128)S(1)} %get-tuple-element.40, f32[12,512]{1,0:T(8,128)S(1)} %copy-done.41, f32[12,512,1024]{2,1,0:T(8,128)} %get-tuple-element.91, pred[1024]{0:T(1024)(128)(4,1)S(1)} %copy-done.63, ...), kind=kLoop, calls=%fused_computation | loop fusion | flops 75497472 | bytes 125928448 | tf_op jit(solution)/shard_map/convert_element_type | solution.py:67
  447.2 12.5 add_convert_fusion.2
  468.8 11.1 fusion.79
  480.0 10.8 fusion.66
  504.8 38.9 %all-reduce.3 = f32[13,768]{1,0:T(8,128)S(1)} all-reduce(f32[13,768]{1,0:T(8,128)S(1)} %concatenate.22), channel_id=7, replica_groups=mesh['dp'=8,'ns'=4] {'dp','ns'}, use_global_device_ids=true, to_apply=%region_35.36.clone | all-reduce | flops 9984 | bytes 79872
  547.3 109.4 %reduce-scatter.14.cloned.1.call-done = f32[768,72]{0,1:T(8,128)} async-done(((f32[768,2304]{0,1:T(8,128)}), f32[768,72]{0,1:T(8,128)}) %reduce-scatter.14.cloned.1.call-update) | async-done | bytes 221200 | tf_op jit(solution)/shard_map/reduce_scatter | solution.py:259
  659.5 138.5 %reduce-scatter.18.cloned.1.call-done = f32[768,96]{0,1:T(8,128)} async-done(((f32[768,3072]{0,1:T(8,128)}), f32[768,96]{0,1:T(8,128)}) %reduce-scatter.18.cloned.1.call-update) | async-done | bytes 294928 | tf_op jit(solution)/shard_map/reduce_scatter | solution.py:260
  800.4 138.5 %reduce-scatter.20.cloned.1.call-done = f32[96,768]{1,0:T(8,128)} async-done(((f32[3072,768]{1,0:T(8,128)}), f32[96,768]{1,0:T(8,128)}) %reduce-scatter.20.cloned.1.call-update) | async-done | bytes 294928 | tf_op jit(solution)/shard_map/reduce_scatter | solution.py:265
  942.4 41.0 %psum.14 = f32[]{:T(128)} all-reduce(f32[]{:T(128)S(6)} %reduce_sum.349), channel_id=1, replica_groups=mesh['dp'=8,'ns'=4] {'dp','ns'}, use_global_device_ids=true, to_apply=%region_37.38 | all-reduce | flops 1 | bytes 8 | tf_op jit(solution)/shard_map/psum | solution.py:272
  993.4 39.4 %psum.15 = f32[4]{0:T(128)S(1)} all-reduce(f32[4]{0:T(128)S(1)} %pad_maximum_fusion.9), channel_id=1, replica_groups=mesh['dp'=8,'ns'=4] {'dp','ns'}, use_global_device_ids=true, to_apply=%region_42.43 | all-reduce | flops 4 | bytes 32 | tf_op jit(solution)/shard_map/psum | solution.py:282
  1046.3 134.5 %reduce-scatter.22.cloned.1.call-done = f32[4,24,768]{2,1,0:T(8,128)} async-done(((f32[4,768,768]{2,1,0:T(8,128)}), f32[4,24,768]{2,1,0:T(8,128)}) %reduce-scatter.22.cloned.1.call-update) | async-done | bytes 294928 | tf_op jit(solution)/shard_map/reduce_scatter | solution.py:297
  1180.8 86.3 %all-gather.19.cloned.1.call-done = f32[4,768,768]{2,1,0:T(8,128)} async-done(((f32[4,24,768]{2,1,0:T(8,128)}), f32[4,768,768]{2,1,0:T(8,128)}) %all-gather.19.cloned.1.call-update) | async-done | bytes 9437200 | tf_op jit(solution)/shard_map/all_gather | solution.py:298
  1292.2 131.9 %reduce-scatter.24.cloned.1.call-done = f32[4,24,768]{2,1,0:T(8,128)} async-done(((f32[4,768,768]{2,1,0:T(8,128)}), f32[4,24,768]{2,1,0:T(8,128)}) %reduce-scatter.24.cloned.1.call-update) | async-done | bytes 294928 | tf_op jit(solution)/shard_map/reduce_scatter | solution.py:297
  1424.2 86.8 %all-gather.21.cloned.1.call-done = f32[4,768,768]{2,1,0:T(8,128)} async-done(((f32[4,24,768]{2,1,0:T(8,128)}), f32[4,768,768]{2,1,0:T(8,128)}) %all-gather.21.cloned.1.call-update) | async-done | bytes 9437200 | tf_op jit(solution)/shard_map/all_gather | solution.py:298
  1536.0 131.9 %reduce-scatter.26.cloned.1.call-done = f32[4,24,768]{2,1,0:T(8,128)} async-done(((f32[4,768,768]{2,1,0:T(8,128)}), f32[4,24,768]{2,1,0:T(8,128)}) %reduce-scatter.26.cloned.1.call-update) | async-done | bytes 294928 | tf_op jit(solution)/shard_map/reduce_scatter | solution.py:297
  1668.0 86.2 %all-gather.23.cloned.1.call-done = f32[4,768,768]{2,1,0:T(8,128)} async-done(((f32[4,24,768]{2,1,0:T(8,128)}), f32[4,768,768]{2,1,0:T(8,128)}) %all-gather.23.cloned.1.call-update) | async-done | bytes 9437200 | tf_op jit(solution)/shard_map/all_gather | solution.py:298
  1779.5 132.0 %reduce-scatter.28.cloned.1.call-done = f32[4,24,768]{2,1,0:T(8,128)} async-done(((f32[4,768,768]{2,1,0:T(8,128)}), f32[4,24,768]{2,1,0:T(8,128)}) %reduce-scatter.28.cloned.1.call-update) | async-done | bytes 294928 | tf_op jit(solution)/shard_map/reduce_scatter | solution.py:297
  1911.5 86.5 %all-gather.25.cloned.1.call-done = f32[4,768,768]{2,1,0:T(8,128)} async-done(((f32[4,24,768]{2,1,0:T(8,128)}), f32[4,768,768]{2,1,0:T(8,128)}) %all-gather.25.cloned.1.call-update) | async-done | bytes 9437200 | tf_op jit(solution)/shard_map/all_gather | solution.py:298
  2023.2 131.8 %reduce-scatter.30.cloned.1.call-done = f32[4,24,768]{2,1,0:T(8,128)} async-done(((f32[4,768,768]{2,1,0:T(8,128)}), f32[4,24,768]{2,1,0:T(8,128)}) %reduce-scatter.30.cloned.1.call-update) | async-done | bytes 294928 | tf_op jit(solution)/shard_map/reduce_scatter | solution.py:297
  2161.1 80.3 %all-gather.27.cloned.1.call-done = f32[4,768,768]{2,1,0:T(8,128)} async-done(((f32[4,24,768]{2,1,0:T(8,128)}), f32[4,768,768]{2,1,0:T(8,128)}) %all-gather.27.cloned.1.call-update) | async-done | bytes 9437200 | tf_op jit(solution)/shard_map/all_gather | solution.py:298
  (308 shorter events, 288.3 us)
Async XLA Ops:
  7.2 97.6 %all-gather.11.cloned.1.call-start = ((), (), s32[]{:S(2)}) async-start(), calls=%async_computation.10 | async-start | bytes 3649536 | tf_op jit(solution)/shard_map/all_gather | solution.py:123
  9.0 180.3 %all-gather.13.cloned.1.call-start = ((), (), s32[]{:S(2)}) async-start(), calls=%async_computation.11 | async-start | bytes 1216512 | tf_op jit(solution)/shard_map/all_gather | solution.py:128
  10.6 186.4 %all-gather.15.cloned.1.call-start = ((), (), s32[]{:S(2)}) async-start(), calls=%async_computation.12 | async-start | bytes 4866048 | tf_op jit(solution)/shard_map/all_gather | solution.py:124
  12.3 250.5 %all-gather.17.cloned.1.call-start = ((), (), s32[]{:S(2)}) async-start(), calls=%async_computation.13 | async-start | bytes 4866048 | tf_op jit(solution)/shard_map/all_gather | solution.py:129
  14.0 530.5 %reduce-scatter.32.cloned.1.call-start = ((), (), s32[]{:S(2)}) async-start(), calls=%async_computation.28 | async-start | bytes 405504
  59.4 129.9 %copy-start.46 = (f32[768]{0:T(1024)}, f32[768]{0:T(1024)S(1)}, u32[]{:S(2)}) copy-start(f32[768]{0:T(1024)S(1)} %get-tuple-element.39) | copy-start | bytes 9220
  59.4 137.5 %copy-start.69 = (f32[768]{0:T(1024)}, f32[768]{0:T(1024)S(1)}, u32[]{:S(2)}) copy-start(f32[768]{0:T(1024)S(1)} %get-tuple-element.32) | copy-start | bytes 9220
  60.1 117.5 %copy-start.62 = (pred[1024]{0:T(1024)(128)(4,1)}, pred[1024]{0:T(1024)(128)(4,1)S(1)}, u32[]{:S(2)}) copy-start(pred[1024]{0:T(1024)(128)(4,1)S(1)} %iota_compare_fusion) | copy-start | bytes 3076
  62.1 127.2 %copy-start.52 = (pred[1024]{0:T(1024)(128)(4,1)}, pred[1024]{0:T(1024)(128)(4,1)S(1)}, u32[]{:S(2)}) copy-start(pred[1024]{0:T(1024)(128)(4,1)S(1)} %get-tuple-element.73) | copy-start | bytes 3076
  197.0 65.8 %copy-start.14 = (f32[1024,768]{1,0:T(8,128)S(1)}, f32[1024,768]{1,0:T(8,128)}, u32[]{:S(2)}) copy-start(f32[1024,768]{1,0:T(8,128)} %copy-done.13) | copy-start | bytes 9437188
  197.0 65.8 %copy-start.73 = (f32[768]{0:T(1024)S(1)}, f32[768]{0:T(1024)}, u32[]{:S(2)}) copy-start(f32[768]{0:T(1024)} %get-tuple-element.31) | copy-start | bytes 9220
  277.2 268.6 %reduce-scatter.16.cloned.1.call-start = ((), (), s32[]{:S(2)}) async-start(), calls=%async_computation.15 | async-start | bytes 2433024 | tf_op jit(solution)/shard_map/reduce_scatter | solution.py:264
  436.9 219.8 %reduce-scatter.14.cloned.1.call-start = ((), (), s32[]{:S(2)}) async-start(), calls=%async_computation.14 | async-start | bytes 7299072 | tf_op jit(solution)/shard_map/reduce_scatter | solution.py:259
  468.2 329.9 %reduce-scatter.18.cloned.1.call-start = ((), (), s32[]{:S(2)}) async-start(), calls=%async_computation.16 | async-start | bytes 9732096 | tf_op jit(solution)/shard_map/reduce_scatter | solution.py:260
  480.0 458.9 %reduce-scatter.20.cloned.1.call-start = ((), (), s32[]{:S(2)}) async-start(), calls=%async_computation.17 | async-start | bytes 9732096 | tf_op jit(solution)/shard_map/reduce_scatter | solution.py:265
  490.8 689.9 %reduce-scatter.22.cloned.1.call-start = ((), (), s32[]{:S(2)}) async-start(), calls=%async_computation.18 | async-start | bytes 9732096 | tf_op jit(solution)/shard_map/reduce_scatter | solution.py:297
  501.4 482.8 %copy-start.38 = (f32[96,768]{1,0:T(8,128)S(1)}, f32[96,768]{1,0:T(8,128)}, u32[]{:S(2)}) copy-start(f32[96,768]{1,0:T(8,128)} %param.31) | copy-start | bytes 884740
  504.5 481.3 %copy-start.39 = (f32[768,96]{0,1:T(8,128)S(1)}, f32[768,96]{0,1:T(8,128)}, u32[]{:S(2)}) copy-start(f32[768,96]{0,1:T(8,128)} %param.30) | copy-start | bytes 884740
  504.5 483.1 %copy-start.45 = (f32[24,768]{1,0:T(8,128)S(1)}, f32[24,768]{1,0:T(8,128)}, u32[]{:S(2)}) copy-start(f32[24,768]{1,0:T(8,128)} %param.29) | copy-start | bytes 221188
  504.5 484.6 %copy-start.43 = (f32[768,72]{0,1:T(8,128)S(1)}, f32[768,72]{0,1:T(8,128)}, u32[]{:S(2)}) copy-start(f32[768,72]{0,1:T(8,128)} %param.28) | copy-start | bytes 663556
  543.8 443.8 %copy-start.44 = (f32[13,768]{1,0:T(8,128)}, f32[13,768]{1,0:T(8,128)S(1)}, u32[]{:S(2)}) copy-start(f32[13,768]{1,0:T(8,128)S(1)} %all-reduce.3) | copy-start | bytes 119812
  985.8 60.4 %copy-start.32 = (f32[96,768]{1,0:T(8,128)}, f32[96,768]{1,0:T(8,128)S(1)}, u32[]{:S(2)}) copy-start(f32[96,768]{1,0:T(8,128)S(1)} %get-tuple-element.67) | copy-start | bytes 884740
  987.5 58.6 %copy-start.33 = (f32[768,96]{0,1:T(8,128)}, f32[768,96]{0,1:T(8,128)S(1)}, u32[]{:S(2)}) copy-start(f32[768,96]{0,1:T(8,128)S(1)} %get-tuple-element.65) | copy-start | bytes 884740
  1046.2 220.9 %all-gather.19.cloned.1.call-start = ((), (), s32[]{:S(2)}) async-start(), calls=%async_computation.19 | async-start | bytes 9732096 | tf_op jit(solution)/shard_map/all_gather | solution.py:298
  1180.8 243.3 %reduce-scatter.24.cloned.1.call-start = ((), (), s32[]{:S(2)}) async-start(), calls=%async_computation.20 | async-start | bytes 9732096 | tf_op jit(solution)/shard_map/reduce_scatter | solution.py:297
  1292.1 218.8 %all-gather.21.cloned.1.call-start = ((), (), s32[]{:S(2)}) async-start(), calls=%async_computation.21 | async-start | bytes 9732096 | tf_op jit(solution)/shard_map/all_gather | solution.py:298
  1424.1 243.8 %reduce-scatter.26.cloned.1.call-start = ((), (), s32[]{:S(2)}) async-start(), calls=%async_computation.22 | async-start | bytes 9732096 | tf_op jit(solution)/shard_map/reduce_scatter | solution.py:297
  1536.0 218.2 %all-gather.23.cloned.1.call-start = ((), (), s32[]{:S(2)}) async-start(), calls=%async_computation.23 | async-start | bytes 9732096 | tf_op jit(solution)/shard_map/all_gather | solution.py:298
  1668.0 243.5 %reduce-scatter.28.cloned.1.call-start = ((), (), s32[]{:S(2)}) async-start(), calls=%async_computation.24 | async-start | bytes 9732096 | tf_op jit(solution)/shard_map/reduce_scatter | solution.py:297
  1779.4 218.6 %all-gather.25.cloned.1.call-start = ((), (), s32[]{:S(2)}) async-start(), calls=%async_computation.25 | async-start | bytes 9732096 | tf_op jit(solution)/shard_map/all_gather | solution.py:298
  1911.5 243.6 %reduce-scatter.30.cloned.1.call-start = ((), (), s32[]{:S(2)}) async-start(), calls=%async_computation.26 | async-start | bytes 9732096 | tf_op jit(solution)/shard_map/reduce_scatter | solution.py:297
  2023.0 218.4 %all-gather.27.cloned.1.call-start = ((), (), s32[]{:S(2)}) async-start(), calls=%async_computation.27 | async-start | bytes 9732096 | tf_op jit(solution)/shard_map/all_gather | solution.py:298
  (65 other events, 834.3 us)
Sparse Core Ops, SparseCore 0:
  11.5 62.8 all-gather.10
  77.9 52.8 all-gather.12
  134.3 62.5 all-gather.14
  200.2 62.4 all-gather.16
  277.3 91.3 reduce-scatter.31
  437.0 95.8 reduce-scatter.15
  538.6 118.0 reduce-scatter.13
  663.6 134.4 reduce-scatter.17
  804.0 134.8 reduce-scatter.19
  1046.3 134.3 reduce-scatter.21
  1183.7 83.3 all-gather.18
  1292.3 131.8 reduce-scatter.23
  1427.5 83.4 all-gather.20
  1536.1 131.7 reduce-scatter.25
  1670.7 83.4 all-gather.22
  1779.5 131.8 reduce-scatter.27
  1914.7 83.3 all-gather.24
  2023.1 131.9 reduce-scatter.29
  2158.0 83.3 all-gather.26
where the time goes:
time: 2270 us
  waiting for transfers between devices  1500 us (66%)
  matrix products  412 us (18%)
  blocking collectives  203 us (9%)
  other arithmetic  101 us (4%)
  between operations  25.1 us (1%)
    reduce_scatter x5, waiting for transfers between devices, spread_total(): lax.psum_scatter(gram_local, ('dp', 'ns'), scatter_dimension=1, tiled=True)  662 us
    all_gather x5, waiting for transfers between devices, spread_total(): return lax.all_gather(gram_rows, ('dp', 'ns'), axis=1, tiled=True)  426 us
    reduce_scatter x1, waiting for transfers between devices, local(): lax.psum_scatter(grad_fc1, ('dp', 'ns'), scatter_dimension=1, tiled=True)  139 us
    reduce_scatter x1, waiting for transfers between devices, local(): lax.psum_scatter(grad_fc2, ('dp', 'ns'), scatter_dimension=0, tiled=True)  138 us
    reduce_scatter x1, waiting for transfers between devices, local(): lax.psum_scatter(grad_qkv, ('dp', 'ns'), scatter_dimension=1, tiled=True)  109 us
    dot_general x5, matrix products, newton_steps(): gram_local = jnp.einsum('mrd,mre->mde', stacked, stacked, precision=highest)  49.9 us
    dot_general x5, matrix products, newton_steps(): jnp.einsum('mrd,mde->mre', stacked, gram_matrix, precision=highest)  46.3 us
    dot_general x2, matrix products, attend_back_span(): jnp.einsum('qhe,khe->hqk', grad_mix, value_rows, preferred_element_type=j...  45.5 us
  transfers between devices with their start and end apart: 19, of which 14 were waited for; matrix products, arithmetic and copies ran while one was open for 16% of the time, Pallas kernels for 0%

commit v1 on v0

v1 whole, which is shorter than its diff:
```python
import functools
import math

import jax
import jax.numpy as jnp
from jax import lax
from jax.experimental import pallas as pl
from jax.experimental.pallas import tpu as pltpu
from jax.sharding import PartitionSpec as P

HEADS = 12
HEAD_DIM = 64
PAYLOAD = 48
STACK = 16
MESH = pl.DeviceIdType.MESH

newton_first = 3.4445
newton_second = -4.775
newton_third = 2.0315
muon_rate = 0.5
muon_decay = 0.01
momentum_keep = 0.5
beta_first = 0.9
beta_second = 0.95
head_rate = 0.1
head_decay = 0.01
vector_rate = 0.3
highest = lax.Precision.HIGHEST
half_type = jnp.bfloat16
both = ("dp", "ns")

def ring_place(index, count):
    high, odd = lax.div(index, 2), lax.rem(index, 2)
    return high + odd * (count - 1 - 2 * high)

def ring_index(place, count):
    late = lax.div(place, count // 2)
    return 2 * place + late * (2 * count - 1 - 4 * place)

class Peers:
    def __init__(self, n_dp, n_ns):
        self.n_dp, self.n_ns = n_dp, n_ns
        self.dp, self.ns = lax.axis_index("dp"), lax.axis_index("ns")
        place = ring_place(self.dp, n_dp)
        low = lax.rem(self.ns, 2)
        high = lax.rem(lax.div(self.ns, 2), 2)
        flips = (0, 1 - 2 * low, 2 - 4 * high)
        self.columns = [self.ns, self.ns + flips[1], self.ns + flips[2], self.ns + flips[1] + flips[2]]
        self.rows = {0: self.dp}
        for shift in range(-(n_dp // 2), (n_dp - 1) // 2 + 1):
            if shift:
                self.rows[shift] = ring_index(lax.rem(place + shift + n_dp, n_dp), n_dp)
        self.ways = {
            "right": (self.rows[1], self.ns),
            "left": (self.rows[-1], self.ns),
            "cross": (self.dp, self.columns[2]),
            "core": (self.dp, self.columns[1]),
        }

    def slot(self, shift, bit):
        return self.rows[shift] * self.n_ns + self.columns[bit]

    def device(self, way):
        return self.ways[way]

    def greet(self):
        barrier = pltpu.get_barrier_semaphore()
        for way in ("right", "left", "cross", "core"):
            pl.semaphore_signal(barrier, inc=1, device_id=self.device(way), device_id_type=MESH)
        pl.semaphore_wait(barrier, 4)

def routes(n_dp, mode):
    ring_first, dp_only = mode != "cross", mode == "dp"
    right, left = n_dp // 2, (n_dp - 1) // 2
    table = {}
    start = [("right", ("r", 1, 0)), ("left", ("l", 1, 0)), ("cross", ("x", 0, 2)), ("core", ("c", 0, 1))]
    if dp_only:
        start = start[:2]
    columns = (0,) if ring_first else (0, 2)

    def along(kind, step, bit):
        shift = -step if kind == "r" else step
        limit = right if kind == "r" else left
        out = []
        if step < limit:
            out.append(("right" if kind == "r" else "left", (kind, step + 1, bit)))
        if not dp_only:
            if ring_first:
                out.append(("cross", ("x", shift, 2)))
            out.append(("core", ("c", shift, bit ^ 1)))
        table[(kind, step, bit)] = (shift, bit, out)

    def crossed(shift):
        out = []
        if dp_only:
            return
        if not ring_first:
            out += [("right", ("r", 1, 2)), ("left", ("l", 1, 2))]
        out.append(("core", ("c", shift, 3)))
        table[("x", shift, 2)] = (shift, 2, out)

    for step in range(1, right + 2):
        if ring_first or step == 1:
            if step == 1:
                crossed(0)
            else:
                crossed(1 - step)
                if step - 1 <= left:
                    crossed(step - 1)
        for bit in columns:
            if step <= right:
                along("r", step, bit)
            if step <= left:
                along("l", step, bit)
    return start, table

def finals(n_dp, mode):
    if mode == "dp":
        return []
    right, left = n_dp // 2, (n_dp - 1) // 2
    shifts = [0]
    for step in range(1, right + 1):
        shifts.append(-step)
        if step <= left:
            shifts.append(step)
    return [(shift, bit) for shift in shifts for bit in (1, 3)]

def gather_kernel(n_dp, n_ns, orders, *refs):
    count = len(orders)
    blocks, outs = refs[:count], refs[count : 2 * count]
    send_sem, recv_sem, own_sem = refs[2 * count :]
    peers = Peers(n_dp, n_ns)
    peers.greet()
    sends = []
    plans = [routes(n_dp, order) for order in orders]
    names = []
    for (start, table), mode in zip(plans, orders):
        ids = {}
        for key in table:
            ids[key] = len(ids)
        for shift, bit in finals(n_dp, mode):
            ids[("c", shift, bit)] = len(ids)
        names.append(ids)

    def push(a, source, slot, way, name):
        copy = pltpu.make_async_remote_copy(
            src_ref=source,
            dst_ref=outs[a].at[slot],
            send_sem=send_sem.at[a, names[a][name]],
            recv_sem=recv_sem.at[a, names[a][name]],
            device_id=peers.device(way),
            device_id_type=MESH,
        )
        copy.start()
        sends.append(copy)

    def landed(a, slot, name):
        pltpu.make_async_remote_copy(
            src_ref=outs[a].at[slot],
            dst_ref=outs[a].at[slot],
            send_sem=send_sem.at[a, names[a][name]],
            recv_sem=recv_sem.at[a, names[a][name]],
            device_id=peers.device("core"),
            device_id_type=MESH,
        ).wait_recv()

    def slot_of(a, shift, bit):
        return peers.rows[shift] if orders[a] == "dp" else peers.slot(shift, bit)

    for a in range(count):
        for way, name in plans[a][0]:
            push(a, blocks[a], slot_of(a, 0, 0), way, name)
    local = [
        pltpu.make_async_copy(blocks[a], outs[a].at[slot_of(a, 0, 0)], own_sem.at[a])
        for a in range(count)
    ]
    for copy in local:
        copy.start()
    rows = [list(plan[1].items()) for plan in plans]
    for turn in range(max(len(row) for row in rows)):
        for a in range(count):
            if turn < len(rows[a]):
                name, (shift, bit, out) = rows[a][turn]
                slot = slot_of(a, shift, bit)
                landed(a, slot, name)
                for way, target in out:
                    push(a, outs[a].at[slot], slot, way, target)
    tails = [finals(n_dp, mode) for mode in orders]
    for turn in range(max(len(tail) for tail in tails)):
        for a in range(count):
            if turn < len(tails[a]):
                shift, bit = tails[a][turn]
                landed(a, slot_of(a, shift, bit), ("c", shift, bit))
    for copy in local:
        copy.wait()
    for copy in sends:
        copy.wait_send()

def all_gather(n_dp, n_ns, arrays, orders, collective_id):
    n_dev = n_dp * n_ns
    sizes = [n_dp if mode == "dp" else n_dev for mode in orders]
    return pl.pallas_call(
        functools.partial(gather_kernel, n_dp, n_ns, orders),
        out_shape=tuple(
            jax.ShapeDtypeStruct((size,) + a.shape, a.dtype) for size, a in zip(sizes, arrays)
        ),
        in_specs=[pl.BlockSpec(memory_space=pltpu.VMEM)] * len(arrays),
        out_specs=tuple(pl.BlockSpec(memory_space=pl.ANY) for _ in arrays),
        scratch_shapes=[
            pltpu.SemaphoreType.DMA((len(arrays), n_dev - 1)),
            pltpu.SemaphoreType.DMA((len(arrays), n_dev - 1)),
            pltpu.SemaphoreType.DMA((len(arrays),)),
        ],
        compiler_params=pltpu.CompilerParams(collective_id=collective_id, has_side_effects=True),
    )(*arrays)


def swap_kernel(n_ns, block_ref, out_ref, send_sem, recv_sem, own_sem):
    dp, ns = lax.axis_index("dp"), lax.axis_index("ns")
    others = [lax.rem(ns + step, n_ns) for step in range(1, n_ns)]
    barrier = pltpu.get_barrier_semaphore()
    for other in others:
        pl.semaphore_signal(barrier, inc=1, device_id=(dp, other), device_id_type=MESH)
    pl.semaphore_wait(barrier, n_ns - 1)
    copies = []
    for index, other in enumerate(others):
        copy = pltpu.make_async_remote_copy(
            src_ref=block_ref.at[other],
            dst_ref=out_ref.at[ns],
            send_sem=send_sem.at[index],
            recv_sem=recv_sem.at[index],
            device_id=(dp, other),
            device_id_type=MESH,
        )
        copy.start()
        copies.append(copy)
    own = pltpu.make_async_copy(block_ref.at[ns], out_ref.at[ns], own_sem)
    own.start()
    for index in range(n_ns - 1):
        sender = lax.rem(ns + n_ns - 1 - index, n_ns)
        pltpu.make_async_remote_copy(
            src_ref=block_ref.at[sender],
            dst_ref=out_ref.at[sender],
            send_sem=send_sem.at[index],
            recv_sem=recv_sem.at[index],
            device_id=(dp, sender),
            device_id_type=MESH,
        ).wait_recv()
    own.wait()
    for copy in copies:
        copy.wait_send()


def swap(n_ns, block, collective_id):
    return pl.pallas_call(
        functools.partial(swap_kernel, n_ns),
        out_shape=jax.ShapeDtypeStruct(block.shape, block.dtype),
        in_specs=[pl.BlockSpec(memory_space=pltpu.VMEM)],
        out_specs=pl.BlockSpec(memory_space=pltpu.VMEM),
        scratch_shapes=[
            pltpu.SemaphoreType.DMA((n_ns - 1,)),
            pltpu.SemaphoreType.DMA((n_ns - 1,)),
            pltpu.SemaphoreType.DMA,
        ],
        compiler_params=pltpu.CompilerParams(collective_id=collective_id, has_side_effects=True),
    )(block)


def nn(left, right):
    return lax.dot_general(left, right, (((1,), (0,)), ((), ())), preferred_element_type=jnp.float32)

def nt(left, right):
    return lax.dot_general(left, right, (((1,), (1,)), ((), ())), preferred_element_type=jnp.float32)

def erfc_tail(size):
    t = 1.0 / (1.0 + (0.3275911 * math.sqrt(0.5)) * size)
    poly = ((((1.061405429 * t - 1.453152027) * t + 1.421413741) * t - 0.284496736) * t + 0.254829592) * t
    return poly * jnp.exp(-0.5 * (size * size))

def gelu(value):
    size = jnp.abs(value)
    return jnp.maximum(value, 0.0) - (0.5 * size) * erfc_tail(size)

def gelu_slope(value):
    tail = 0.5 * erfc_tail(jnp.abs(value))
    cdf = jnp.where(value >= 0.0, 1.0 - tail, tail)
    return cdf + value * (jnp.exp(-0.5 * value * value) * (1.0 / math.sqrt(2.0 * math.pi)))

def center_rows(rows):
    scale = 1.0 / rows.shape[1]
    center = rows - jnp.sum(rows, axis=1, keepdims=True) * scale
    spread = jnp.sum(center * center, axis=1, keepdims=True) * scale
    inverse = lax.rsqrt(spread + 1e-06)
    return center * inverse, inverse

def norm_back(grad_rows, normed, inverse, gain):
    scale = 1.0 / grad_rows.shape[1]
    scaled = grad_rows * gain
    first_mean = jnp.sum(scaled, axis=1, keepdims=True) * scale
    second_mean = jnp.sum(scaled * normed, axis=1, keepdims=True) * scale
    return inverse * (scaled - first_mean - normed * second_mean)

def thirds(wide):
    high = wide.astype(half_type).astype(jnp.float32)
    rest = wide - high
    mid = rest.astype(half_type).astype(jnp.float32)
    return high, mid, rest - mid

def stack_row(row):
    high, mid, low = thirds(row)
    place = lax.broadcasted_iota(jnp.int32, (STACK, row.shape[1]), 0)
    tall = jnp.where(place == 0, high, jnp.where(place == 1, mid, jnp.where(place == 2, low, 0.0)))
    return tall.astype(half_type)

def row_nn(row, matrix):
    return jnp.sum(nn(stack_row(row), matrix), axis=0, keepdims=True)

def row_nt(row, matrix):
    return jnp.sum(nt(stack_row(row), matrix), axis=0, keepdims=True)

def stack_wide(wide):
    return jnp.concatenate([piece.astype(half_type) for piece in thirds(wide)], axis=0)

def wide_nn(wide, matrix):
    tall = nn(stack_wide(wide), matrix)
    n = wide.shape[0]
    return tall[:n] + tall[n : 2 * n] + tall[2 * n :]

def wide_nt(wide, matrix):
    tall = nt(stack_wide(wide), matrix)
    n = wide.shape[0]
    return tall[:n] + tall[n : 2 * n] + tall[2 * n :]

def model_kernel(block, counts_ref, patches_ref, mask_col_ref, mask_row_ref, hog_ref, vec_ref,
                 qkv_ref, out_ref, fc1_ref, fc2_ref, head_ref,
                 hidden_ref, patch_grad_ref, payload_ref, query_ref, input_ref,
                 in1, joined, mixture, value_ext, bias_ref, after_rep, pre_rep, act_rep, in2_rep, grad_one_ref):
    seq, width = patches_ref.shape
    ff = fc1_ref.shape[0]
    steps = seq // block
    ff_rows = ff // width

    def span(step):
        return pl.ds(pl.multiple_of(step * block, block), block)

    def vec(index):
        return vec_ref[pl.ds(index, 1), :]

    place_row = lax.broadcasted_iota(jnp.int32, (1, seq), 1)
    live_row = place_row < counts_ref[0]
    bias_ref[...] = jnp.where(live_row, 0.0, -1e30)

    def stream_of(where):
        return jnp.where(mask_col_ref[where, :] == 1, vec(8), patches_ref[where, :].astype(jnp.float32))

    def first_step(step, carry):
        where = span(step)
        normed, _ = center_rows(stream_of(where))
        rows = (normed * vec(0) + vec(1)).astype(half_type)
        in1[where, :] = rows
        for part in range(3):
            piece = nt(rows, qkv_ref[pl.ds(part * width, width), :])
            if part == 0:
                piece = piece + vec(2)
            if part == 2:
                piece = piece + vec(3)
            joined[where, pl.ds(part * width, width)] = piece.astype(half_type)
        return carry

    lax.fori_loop(0, steps, first_step, 0)
    lane = lax.broadcasted_iota(jnp.int32, (block, 128), 1)

    def pair_step(pair, carry):
        cols = pl.multiple_of(pair * 128, 128)
        values = joined[:, pl.ds(2 * width + cols, 128)]
        keys = joined[:, pl.ds(width + cols, 128)]

        def attend(step, inner):
            where = span(step)
            query = joined[where, pl.ds(cols, 128)] * jnp.asarray(0.125, half_type)
            parts = []
            for side in range(2):
                own = (lane < 64) if side == 0 else (lane >= 64)
                scores = nt(jnp.where(own, query, jnp.zeros_like(query)), keys) + bias_ref[...]
                raised = jnp.exp(scores - jnp.max(scores, axis=1, keepdims=True))
                weights = raised * (1.0 / jnp.sum(raised, axis=1, keepdims=True))
                parts.append(nn(weights.astype(half_type), values))
            mixture[where, pl.ds(cols, 128)] = jnp.where(lane < 64, parts[0], parts[1]).astype(half_type)
            return inner

        return lax.fori_loop(0, steps, attend, carry)

    lax.fori_loop(0, width // 128, pair_step, 0)

    def mlp_step(step, carry):
        where = span(step)
        rep = pl.ds(pl.multiple_of(step * 16, 16), 16)
        after = stream_of(where) + (nn(mixture[where, :], out_ref[...]) + vec(4))
        after_rep[rep, :] = after[:16]
        normed, _ = center_rows(after)
        rows = (normed * vec(5) + vec(6)).astype(half_type)
        in2_rep[rep, :] = rows[:16]
        total = after + vec(7)
        for part in range(ff_rows):
            chunk = pl.ds(part * width, width)
            pre = nt(rows, fc1_ref[chunk, :]) + vec(9 + part)
            pre_rep[rep, chunk] = pre[:16]
            act = gelu(pre).astype(half_type)
            act_rep[rep, chunk] = act[:16]
            total = total + nn(act, fc2_ref[chunk, :])
        hidden_ref[where, :] = total.astype(half_type)
        return carry

    lax.fori_loop(0, steps, mlp_step, 0)

    hid_rep = hidden_ref[pl.ds(0, 16), :][:1].astype(jnp.float32)
    chosen = jnp.logical_and(mask_row_ref[...] == 1, live_row).astype(jnp.float32)
    count = jnp.sum(chosen, axis=1, keepdims=True)
    targets = row_nt(chosen, hog_ref[...])
    predicted = row_nn(hid_rep, head_ref[...])
    hog = hog_ref.shape[0]
    grad_pred = 2.0 * (predicted[:, :hog] - targets / count)
    grad_pred = jnp.concatenate([grad_pred, jnp.zeros((1, head_ref.shape[1] - hog), jnp.float32)], axis=1)
    grad_stream = row_nt(grad_pred, head_ref[...])
    grad_act = row_nt(grad_stream, fc2_ref[...])
    grad_pre = grad_act * gelu_slope(pre_rep[pl.ds(0, 16), :][:1])
    grad_two = row_nn(grad_pre, fc1_ref[...])
    norm_two, inverse_two = center_rows(after_rep[pl.ds(0, 16), :][:1])
    grad_attn = grad_stream + norm_back(grad_two, norm_two, inverse_two, vec(5))
    grad_mix = row_nt(grad_attn, out_ref[...])

    head_of = lax.broadcasted_iota(jnp.int32, (STACK, width), 1) // HEAD_DIM
    head_row = lax.broadcasted_iota(jnp.int32, (STACK, width), 0)
    own_head = head_of == head_row
    keys = joined[:, pl.ds(width, width)]
    values = joined[:, pl.ds(2 * width, width)]
    query_rep = joined[pl.ds(0, 16), pl.ds(0, width)][:1].astype(jnp.float32)
    query_heads = jnp.where(own_head, query_rep, 0.0)
    mix_heads = jnp.where(own_head, grad_mix, 0.0)
    scores = nt(query_heads.astype(half_type), keys) * 0.125 + bias_ref[...]
    raised = jnp.exp(scores - jnp.max(scores, axis=1, keepdims=True))
    probs = raised / jnp.sum(raised, axis=1, keepdims=True)
    probs_low = probs.astype(half_type)
    grad_probs = wide_nt(mix_heads, values)
    inner_sum = jnp.sum(probs * grad_probs, axis=1, keepdims=True)
    grad_scores = probs * (grad_probs - inner_sum)
    ds_high, ds_mid, ds_low = thirds(grad_scores)
    ds_stack = stack_wide(grad_scores)
    tall = nn(ds_stack, keys)
    grad_query = jnp.sum(
        jnp.where(own_head, tall[:16] + tall[16:32] + tall[32:], 0.0), axis=0, keepdims=True
    ) * 0.125
    sides = nn(jnp.concatenate([ds_stack, probs_low], axis=0), in1[...])
    key_side = sides[:16] + sides[16:32] + sides[32:48]
    value_side = sides[48:]
    key_back = nn(query_heads.astype(half_type), qkv_ref[pl.ds(width, width), :]) * 0.125
    value_back = wide_nn(mix_heads, qkv_ref[pl.ds(2 * width, width), :])
    query_back = row_nn(grad_query, qkv_ref[pl.ds(0, width), :])
    kb_high, kb_mid, _ = thirds(key_back)
    vb_high, vb_mid, _ = thirds(value_back)
    probs_wide = probs_low.astype(jnp.float32)
    slab = jnp.concatenate(
        [ds_high, ds_high, ds_mid, probs_wide, probs_wide, jnp.zeros((48, seq), jnp.float32)], axis=0
    )
    turned = slab.T.astype(half_type)
    backs = jnp.concatenate(
        [kb_high, kb_mid, kb_high, vb_high, vb_mid, jnp.zeros((48, width), jnp.float32)], axis=0
    ).astype(half_type)
    for part in range(steps):
        grad_one_ref[pl.ds(part * block, block), :] = nn(turned[part * block : (part + 1) * block], backs)

    def last_step(step, carry):
        gain_sum, shift_sum, rep_sum = carry
        where = span(step)
        normed, inverse = center_rows(stream_of(where))
        grad_one = grad_one_ref[where, :]
        mask = mask_col_ref[where, :] == 1
        patch_grad_ref[where, :] = jnp.where(mask, 0.0, norm_back(grad_one, normed, inverse, vec(0)))
        gain_sum = gain_sum + jnp.sum(grad_one * normed, axis=0, keepdims=True)
        shift_sum = shift_sum + jnp.sum(grad_one, axis=0, keepdims=True)
        rep_sum = rep_sum + jnp.sum(jnp.where(mask, grad_one, 0.0), axis=0, keepdims=True)
        return gain_sum, shift_sum, rep_sum

    zero = jnp.zeros((1, width), jnp.float32)
    gain_sum, shift_sum, rep_sum = lax.fori_loop(0, steps, last_step, (zero, zero, zero))
    norm_one, inverse_one = center_rows(vec(8))
    grad_gain = gain_sum + query_back * norm_one
    grad_shift = shift_sum + query_back
    grad_token = grad_attn + norm_back(rep_sum + query_back, norm_one, inverse_one, vec(0))
    weight_sum = jnp.sum(probs_wide, axis=1, keepdims=True)
    value_bias = jnp.sum(jnp.where(own_head, weight_sum, 0.0), axis=0, keepdims=True) * grad_mix
    act_row = act_rep[pl.ds(0, 16), :][:1].astype(jnp.float32)
    pieces = [
        hid_rep,
        jnp.concatenate([grad_pred, jnp.zeros((1, width - grad_pred.shape[1]), jnp.float32)], axis=1),
    ]
    pieces += [act_row[:, part * width : (part + 1) * width] for part in range(ff_rows)]
    pieces += [grad_stream, in2_rep[pl.ds(0, 16), :][:1].astype(jnp.float32)]
    pieces += [grad_pre[:, part * width : (part + 1) * width] for part in range(ff_rows)]
    pieces += [mixture[pl.ds(0, 16), :][:1].astype(jnp.float32), grad_attn, grad_query, grad_mix]
    pieces += [key_side[:HEADS], value_side[:HEADS]]
    pieces += [grad_gain, grad_shift, grad_two * norm_two, grad_two, grad_token, value_bias]
    rows = sum(piece.shape[0] for piece in pieces)
    pieces += [jnp.zeros((PAYLOAD - rows, width), jnp.float32)]
    payload_ref[...] = jnp.concatenate(pieces, axis=0).astype(payload_ref.dtype)
    query_ref[...] = query_rep
    input_ref[...] = in1[pl.ds(0, 16), :][:1].astype(jnp.float32)

def run_model(counts, patches, mask_col, mask_row, hog, vec, qkv, out, fc1, fc2, head, block=256):
    seq, width = patches.shape
    ff = fc1.shape[0]
    vm = pl.BlockSpec(memory_space=pltpu.VMEM)
    rep = (seq // block) * 16
    return pl.pallas_call(
        functools.partial(model_kernel, block),
        out_shape=(
            jax.ShapeDtypeStruct((seq, width), half_type),
            jax.ShapeDtypeStruct((seq, width), jnp.float32),
            jax.ShapeDtypeStruct((PAYLOAD, width), half_type),
            jax.ShapeDtypeStruct((1, width), jnp.float32),
            jax.ShapeDtypeStruct((1, width), jnp.float32),
        ),
        in_specs=[pl.BlockSpec(memory_space=pltpu.SMEM)] + [vm] * 10,
        out_specs=(vm,) * 5,
        scratch_shapes=[
            pltpu.VMEM((seq, width), half_type),
            pltpu.VMEM((seq, 3 * width), half_type),
            pltpu.VMEM((seq, width), half_type),
            pltpu.VMEM((seq, 256), half_type),
            pltpu.VMEM((1, seq), jnp.float32),
            pltpu.VMEM((rep, width), jnp.float32),
            pltpu.VMEM((rep, ff), jnp.float32),
            pltpu.VMEM((rep, ff), half_type),
            pltpu.VMEM((rep, width), half_type),
            pltpu.VMEM((seq, width), jnp.float32),
        ],
        compiler_params=pltpu.CompilerParams(vmem_limit_bytes=63 * 1024 * 1024),
    )(counts, patches, mask_col, mask_row, hog, vec, qkv, out, fc1, fc2, head)


def put_split(ref, value, count, rows=slice(None)):
    for index in range(count):
        piece = value.astype(half_type)
        ref[index, rows, :] = piece
        if index + 1 < count:
            value = value - piece.astype(jnp.float32)

pairs_of = {3: ((0, 1), (1, 0), (0, 0)), 6: ((0, 2), (2, 0), (1, 1), (0, 1), (1, 0), (0, 0))}

def strip_product(left, right, passes, row, tile, col0, width):
    total = None
    for li, ri in pairs_of[passes]:
        part = jnp.dot(left[li, pl.ds(row, tile), :], right[ri, :, pl.ds(col0, width - col0)],
                       preferred_element_type=jnp.float32)
        total = part if total is None else total + part
    return total

def newton_kernel(sym, plan, gram_ref, out_ref, gram_s, poly_s, half_s, total_s, gram_f, work_f, poly_f):
    width = gram_ref.shape[0]
    tile = 256
    def product(left, right, dest, passes, post):
        for r in range(0, width, tile):
            c0 = r if sym else 0
            blk = strip_product(left, right, passes, r, tile, c0, width)
            dest[pl.ds(r, tile), pl.ds(c0, width - c0)] = post(blk, r, c0)
        if sym:
            for r in range(0, width, tile):
                for c in range(r + tile, width, tile):
                    dest[pl.ds(c, tile), pl.ds(r, tile)] = dest[pl.ds(r, tile), pl.ds(c, tile)].T
    gram_f[...] = gram_ref[...]
    for turn in range(5):
        p1 = plan[turn]
        n = 3 if p1 == 6 else 2
        put_split(gram_s, gram_f[...], n)
        def poly_post(blk, r, c0):
            g = gram_f[pl.ds(r, tile), pl.ds(c0, width - c0)]
            rows = lax.broadcasted_iota(jnp.int32, blk.shape, 0) + r
            cols = lax.broadcasted_iota(jnp.int32, blk.shape, 1) + c0
            return newton_third * blk + newton_second * g + jnp.where(rows == cols, newton_first, 0.0)
        product(gram_s, gram_s, poly_f, p1, poly_post)
        put_split(poly_s, poly_f[...], n)
        same = lambda blk, r, c0: blk
        if turn == 0:
            put_split(total_s, poly_f[...], 2)
        else:
            product(total_s, poly_s, work_f, 3, same)
            if turn < 4:
                put_split(total_s, work_f[...], 2)
            else:
                out_ref[...] = work_f[...]
        if turn < 4:
            product(poly_s, gram_s, work_f, p1, same)
            put_split(half_s, work_f[...], n)
            product(half_s, poly_s, gram_f, p1, same)

def newton(gram, sym=True, plan=(6,3,3,3,3)):
    w = gram.shape[0]
    return pl.pallas_call(
        functools.partial(newton_kernel, sym, plan),
        out_shape=jax.ShapeDtypeStruct((w, w), jnp.float32),
        in_specs=[pl.BlockSpec(memory_space=pltpu.VMEM)],
        out_specs=pl.BlockSpec(memory_space=pltpu.VMEM),
        scratch_shapes=[pltpu.VMEM((3, w, w), half_type)] * 3 + [pltpu.VMEM((2, w, w), half_type)]
        + [pltpu.VMEM((w, w), jnp.float32)] * 3,
        compiler_params=pltpu.CompilerParams(vmem_limit_bytes=60 * 1024 * 1024),
    )(gram)


def adam_update(weight, first_old, second_old, grad_piece, rate, decay):
    first_new = beta_first * first_old + (1.0 - beta_first) * grad_piece
    second_new = beta_second * second_old + (1.0 - beta_second) * grad_piece * grad_piece
    weight_new = weight - rate * (first_new / (jnp.sqrt(second_new) + 1e-08) + decay * weight)
    return (first_new, second_new, weight_new)


def exact(spec, left, right):
    return jnp.einsum(spec, left, right, precision=highest)


def local(
    n_dp,
    n_ns,
    patches,
    masked,
    counts,
    hog_targets,
    qkv_weight,
    out_weight,
    fc1_weight,
    fc2_weight,
    head_weight,
    vectors,
    qkv_moment,
    out_moment,
    fc1_moment,
    fc2_moment,
    head_first,
    head_second,
    vector_first,
    vector_second,
):
    n_dev = n_dp * n_ns
    me_dp = lax.axis_index("dp")
    me_ns = lax.axis_index("ns")
    me = me_dp * n_ns + me_ns
    width = patches.shape[1]
    hidden_units = fc1_weight.shape[1] * n_dev
    hog_rows = hog_targets.shape[0]
    seq_len = patches.shape[0]
    n_vec = vectors.shape[0]
    slot_rows = max(fc1_weight.shape[1], qkv_weight.shape[1], fc2_weight.shape[0])

    def slot(tall_piece):
        return jnp.pad(tall_piece, ((0, slot_rows - tall_piece.shape[0]), (0, 0)))

    qkv_block = qkv_weight.T.astype(half_type)
    vec_block = jnp.pad(
        vectors.astype(half_type), ((0, 16 - n_vec), (0, 128 - vectors.shape[1]))
    )
    qkv_slots, vec_slots = all_gather(
        n_dp, n_ns, (qkv_block, vec_block), ("cross", "ring"), 1
    )
    head_block = jnp.pad(head_weight.astype(half_type), ((0, 0), (0, 128 - hog_rows)))
    out_slots, fc1_slots, fc2_slots, head_slots = all_gather(
        n_dp,
        n_ns,
        (
            out_weight.astype(half_type),
            fc1_weight.T.astype(half_type),
            fc2_weight.astype(half_type),
            head_block,
        ),
        ("ring", "ring", "cross", "ring"),
        2,
    )
    my_moments = jnp.stack(
        [
            slot(piece.astype(half_type))
            for piece in (qkv_moment.T, out_moment, fc1_moment.T, fc2_moment)
        ]
    )
    swapped = swap(n_ns, my_moments, 3)
    (old_tall,) = all_gather(n_dp, n_ns, (swapped,), ("dp",), 4)
    old_tall = old_tall.reshape(n_dev, slot_rows, width)
    vec_rows = jnp.pad(
        vec_slots[:, :n_vec, : vectors.shape[1]].transpose(1, 0, 2).reshape(n_vec, width),
        ((0, 16 - n_vec), (0, 0)),
    ).astype(jnp.float32)
    hidden, patch_grads, payload, query_rep, input_rep = run_model(
        counts,
        patches,
        masked.reshape(seq_len, 1),
        masked.reshape(1, seq_len),
        hog_targets,
        vec_rows,
        qkv_slots.reshape(3 * width, width),
        out_slots.reshape(width, width),
        fc1_slots.reshape(hidden_units, width),
        fc2_slots.reshape(hidden_units, width),
        head_slots.reshape(width, 128),
    )
    (gathered,) = all_gather(n_dp, n_ns, (payload,), ("ring",), 5)
    gathered = gathered.astype(jnp.float32)
    query_rep = query_rep.reshape(HEADS, HEAD_DIM)
    input_rep = input_rep.reshape(width)
    ff_rows = hidden_units // width
    cursor = [0]

    def take(count):
        start = cursor[0]
        cursor[0] += count
        return gathered[:, start : start + count].reshape(n_dev, count * width)

    all_hid = take(1)
    all_pred = take(1)[:, :hog_rows]
    all_act = take(ff_rows)
    all_branch = take(1)
    all_two = take(1)
    all_pre = take(ff_rows)
    all_mix = take(1)
    all_attn = take(1)
    all_query = jnp.sum(take(1), axis=0)
    all_gmix = take(1)
    all_key = jnp.sum(take(HEADS).reshape(n_dev, HEADS, width), axis=0)
    all_value = take(HEADS).reshape(n_dev, HEADS, width)
    sums = jnp.sum(gathered[:, cursor[0] : cursor[0] + 6], axis=0)
    sum_one = jnp.sum(gathered[:, 2 + ff_rows], axis=0)
    vector_total = jnp.concatenate(
        [
            sums[0:2],
            all_query[None],
            sums[5:6],
            jnp.sum(all_attn, axis=0)[None],
            sums[2:4],
            sum_one[None],
            sums[4:5],
            jnp.sum(all_pre, axis=0).reshape(ff_rows, width),
        ],
        axis=0,
    )
    def pair_square(left, right):
        return jnp.sum(exact("ia,ja->ij", left, left) * exact("ib,jb->ij", right, right))

    query_scaled = query_rep * 0.125
    gmix_heads = all_gmix.reshape(n_dev, HEADS, HEAD_DIM)
    square_total = (
        pair_square(all_hid, all_pred)
        + pair_square(all_act, all_branch)
        + pair_square(all_two, all_pre)
        + pair_square(all_mix, all_attn)
        + jnp.sum(input_rep * input_rep) * jnp.sum(all_query * all_query)
        + jnp.sum(
            jnp.sum(all_key * all_key, axis=1) * jnp.sum(query_scaled * query_scaled, axis=1)
        )
        + jnp.sum(
            exact("iha,jha->hij", all_value, all_value)
            * exact("ihe,jhe->hij", gmix_heads, gmix_heads)
        )
        + jnp.sum(vector_total * vector_total)
    )
    grad_norm = jnp.sqrt(square_total)
    shrink = jnp.minimum(1.0, 1.0 / (grad_norm + 1e-06))

    qkv_left = jnp.concatenate(
        [
            jnp.concatenate([all_query, jnp.zeros((2 * width,), jnp.float32)])[None],
            jnp.pad(
                (jnp.eye(HEADS)[:, :, None] * query_scaled[None]).reshape(HEADS, width),
                ((0, 0), (width, width)),
            ),
            jnp.pad(
                (jnp.eye(HEADS)[None, :, :, None] * gmix_heads[:, None]).reshape(
                    n_dev * HEADS, width
                ),
                ((0, 0), (2 * width, 0)),
            ),
        ],
        axis=0,
    )
    qkv_right = jnp.concatenate(
        [input_rep[None], all_key, all_value.reshape(n_dev * HEADS, width)], axis=0
    )

    def shard(array, size):
        return lax.dynamic_slice_in_dim(array, me * size, size, axis=1)

    qkv_grad = exact("ra,rd->da", shard(qkv_left, qkv_weight.shape[1]), qkv_right)
    out_grad = exact("ra,rd->ad", shard(all_mix, out_weight.shape[0]), all_attn)
    fc1_grad = exact("ra,rd->da", shard(all_pre, fc1_weight.shape[1]), all_two)
    fc2_grad = exact("ra,rd->ad", shard(all_act, fc2_weight.shape[0]), all_branch)
    head_grad = exact("ra,rd->ad", shard(all_hid, head_weight.shape[0]), all_pred)
    vector_grad = shard(vector_total, vectors.shape[1])
    old_moments = (qkv_moment, out_moment, fc1_moment, fc2_moment)
    muon_grads = (qkv_grad, out_grad, fc1_grad, fc2_grad)
    new_moments = tuple(
        (
            momentum_keep * old_mom + shrink * grad_piece
            for old_mom, grad_piece in zip(old_moments, muon_grads)
        )
    )

    def tall_slots(left, right):
        tall = exact("ra,rd->ad", left, right)
        tall = tall.reshape(n_dev, -1, width)
        return jnp.pad(tall, ((0, 0), (0, slot_rows - tall.shape[1]), (0, 0)))

    grad_tall = lax.switch(
        me_ns,
        [
            lambda: tall_slots(qkv_left, qkv_right),
            lambda: tall_slots(all_mix, all_attn),
            lambda: tall_slots(all_pre, all_two),
            lambda: tall_slots(all_act, all_branch),
        ],
    )
    tall = momentum_keep * old_tall.astype(jnp.float32) + shrink * grad_tall
    flat_tall = tall.reshape(n_dev * slot_rows, width)
    gram = exact("rd,re->de", flat_tall, flat_tall)
    moment_norm = jnp.sqrt(jnp.trace(gram))
    scale = 1.0 / (moment_norm + 1e-07)
    newton_poly = newton(gram * (scale * scale))
    mine = lax.dynamic_slice_in_dim(tall, me_dp * n_ns, n_ns, axis=0) * scale
    finished = exact("srd,de->sre", mine, newton_poly)
    finished = swap(n_ns, finished, 6)
    long_sizes = (3 * width, width, hidden_units, hidden_units)
    old_weights = (qkv_weight, out_weight, fc1_weight, fc2_weight)
    updates = (
        finished[0, : qkv_weight.shape[1]].T,
        finished[1, : out_weight.shape[0]],
        finished[2, : fc1_weight.shape[1]].T,
        finished[3, : fc2_weight.shape[0]],
    )
    new_weights = tuple(
        (
            old_weight
            - muon_rate
            * (
                math.sqrt(max(1.0, long_size / width)) * update_piece
                + muon_decay * old_weight
            )
            for old_weight, update_piece, long_size in zip(old_weights, updates, long_sizes)
        )
    )
    head_first_new, head_second_new, head_new = adam_update(
        head_weight, head_first, head_second, shrink * head_grad, head_rate, head_decay
    )
    vector_first_new, vector_second_new, vectors_new = adam_update(
        vectors, vector_first, vector_second, shrink * vector_grad, vector_rate, 0.0
    )
    return (
        hidden,
        patch_grads,
        grad_norm,
        *new_moments,
        *new_weights,
        *(piece.astype(half_type) for piece in new_weights),
        head_first_new,
        head_second_new,
        head_new,
        head_new.astype(half_type),
        vector_first_new,
        vector_second_new,
        vectors_new,
        vectors_new.astype(half_type),
    )


def solution(mesh):
    rows, cols, flat = P(both, None), P(None, both), P(both)
    placed = (
        rows, flat, flat, cols,
        cols, rows, cols, rows, rows, cols,
        cols, rows, cols, rows,
        rows, rows, cols, cols,
    )
    returned = (
        rows, rows, P(),
        cols, rows, cols, rows,
        cols, rows, cols, rows,
        cols, rows, cols, rows,
        rows, rows, rows, rows,
        cols, cols, cols, cols,
    )
    return jax.shard_map(
        functools.partial(local, mesh.shape["dp"], mesh.shape["ns"]),
        mesh=mesh,
        in_specs=placed,
        out_specs=returned,
        check_vma=False,
    )
```

time: 2270 us -> 481 us (0.21)
  waiting for transfers between devices: 1500 us -> 0 us
  matrix products: 412 us -> 47.7 us
  Pallas kernels: 0 us -> 322 us
  blocking collectives: 203 us -> 0 us
  other arithmetic: 101 us -> 52.9 us
    reduce_scatter x9 -> x0, waiting for transfers between devices: 1050 us -> none  [the longest x5 662 us: spread_total(): lax.psum_scatter(gram_local, ('dp', 'ns'), scatter_dimension=1, tiled=True)]
    all_gather x9 -> x0, waiting for transfers between devices: 455 us -> none  [the longest x5 426 us: spread_total(): return lax.all_gather(gram_rows, ('dp', 'ns'), axis=1, tiled=True)]
    dot_general x42 -> x18, matrix products: 412 us -> 47.7 us  [exact(): return jnp.einsum(spec, left, right, precision=highest)]
    pallas_call x0 -> x8, Pallas kernels: none -> 322 us  [the longest x4 168 us: all_gather(): pl.pallas_call(functools.partial(gather_kernel, n_dp, n_ns, orders), out_...]
    all_gather x2 -> x0, blocking collectives: 83.6 us -> none  [the longest x1 43.6 us: local(): lax.all_gather(vectors.astype(half_type), ('dp', 'ns'), axis=1, tiled=True)]
    psum x2 -> x0, blocking collectives: 80.3 us -> none  [the longest x1 41 us: local(): square_total = lax.psum(square_sum, ('dp', 'ns'))]
    unnamed x1 -> x0, blocking collectives: 38.9 us -> none
    convert_element_type x8 -> x12, other arithmetic: 48.6 us -> 13.8 us  [the longest x6 6.85 us: local(): piece.astype(half_type)]
  transfers between devices with their start and end apart: 19 -> 0, of which waited for: 14 -> 0; matrix products, arithmetic and copies ran while one was open for 16% -> 0% of each run, Pallas kernels for 0% -> 0%
where the time goes in v1:
time: 481 us; the launch traced here: 477 us
  Pallas kernels  322 us (67%)
  other arithmetic  52.9 us (11%)
  matrix products  47.7 us (10%)
  local copies, waits for them, and re-layouts  33.4 us (7%)
  loops' own time  11.2 us (2%)
  between operations  9.88 us (2%)
    pallas_call x4, Pallas kernels, all_gather(): pl.pallas_call(functools.partial(gather_kernel, n_dp, n_ns, orders), out_...  168 us
    pallas_call x1, Pallas kernels, run_model(): pl.pallas_call(functools.partial(model_kernel, block), out_shape=(jax.Sha...  75.1 us
    dot_general x18, matrix products, exact(): return jnp.einsum(spec, left, right, precision=highest)  47.7 us
    pallas_call x1, Pallas kernels, newton(): pl.pallas_call(functools.partial(newton_kernel, sym, plan), out_shape=jax...  41.2 us
    pallas_call x2, Pallas kernels, swap(): pl.pallas_call(functools.partial(swap_kernel, n_ns), out_shape=jax.ShapeD...  37.7 us
    another operation x1, local copies, waits for them, and re-layouts  12 us
    add x1, other arithmetic, local(): tall = momentum_keep * old_tall.astype(jnp.float32) + shrink * grad_tall  11.8 us
    another operation x1, loops' own time, local(): lax.switch(me_ns, [lambda: tall_slots(qkv_left, qkv_right), lambda: tall_...  11.2 us

profile of v1, /device:TPU:1, one launch (start us, length us, event | category | flops | bytes accessed | tf_op | source)
XLA Modules:
  0.0 477.0 jit_solution(15087934849163962163)
XLA Ops:
  0.7 1.6 convert_bitcast_fusion.2.refs_1_
  2.3 1.6 convert_element_type.107.refs_2_
  6.8 53.5 %shard_map.354 = (bf16[32,24,768]{2,1,0:T(8,128)(2,1)}, bf16[32,96,768]{2,1,0:T(8,128)(2,1)}, bf16[32,96,768]{2,1,0:T(8,128)(2,1)}, bf16[32,24,128]{2,1,0:T(8,128)(2,1)}) custom-call(bf16[24,768]{1,0:T(8,128)(2,1)} %convert_element_type.104.refs_0_, bf16[96,768]{1,0:T(8,128)(2,1)} %convert_bitcast_fusion.2.refs_1_, ...), custom_call_target="tpu_custom_call" | custom-call | tf_op jit(solution)/shard_map/pallas_call | solution.py:202
  60.3 1.6 convert_bitcast_fusion.4.refs_0_
  63.2 30.9 %shard_map.353 = (bf16[32,72,768]{2,1,0:T(8,128)(2,1)}, bf16[32,16,128]{2,1,0:T(8,128)(2,1)}) custom-call(bf16[72,768]{1,0:T(8,128)(2,1)} %convert_bitcast_fusion.4.refs_0_, bf16[16,128]{1,0:T(8,128)(2,1)} %pad.37.refs_1_), custom_call_target="tpu_custom_call" | custom-call | tf_op jit(solution)/shard_map/pallas_call | solution.py:202
  95.8 1.7 copy.57.mask_col_ref
  98.2 75.1 %shard_map.355 = (bf16[1024,768]{1,0:T(8,128)(2,1)}, f32[1024,768]{1,0:T(8,128)}, bf16[48,768]{1,0:T(8,128)(2,1)}, f32[1,768]{1,0:T(1,128)}, f32[1,768]{1,0:T(1,128)}) custom-call(s32[1]{0:T(128)S(6)} %copy.140.counts_ref, bf16[1024,768]{1,0:T(8,128)(2,1)} %patches_ref.1, s32[1024,1]{1,0:T(8,128)} %copy.57.mask_col_ref, s32[1,1024]{1,0:T(1,128)} %bitcast.161, ...), custom_call_target="tpu_custom_call" | custom-call | tf_op jit(solution)/shard_map/pallas_call | solution.py:514
  173.3 25.6 %shard_map.356 = bf16[32,48,768]{2,1,0:T(8,128)(2,1)} custom-call(bf16[48,768]{1,0:T(8,128)(2,1)} %get-tuple-element.80.refs_0_), custom_call_target="tpu_custom_call" | custom-call | tf_op jit(solution)/shard_map/pallas_call | solution.py:202
  198.9 2.4 convert_element_type.109
  224.4 2.1 broadcast_multiply_fusion
  226.5 2.3 mul.356
  228.8 2.8 select_maximum_fusion
  234.5 2.0 pad_maximum_fusion
  236.7 31.1 %conditional.1 = (f32[32,96,768]{2,1,0:T(8,128)}) conditional(s32[]{:T(128)} %clamp.3, (f32[397,2304]{1,0:T(8,128)}, f32[397,768]{1,0:T(8,128)}) %tuple.20, (f32[32,48,768]{2,1,0:T(8,128)}, f32[32,1,768]{2,1,0:T(1,128)S(1)}) %tuple.63, (f32[32,4,768]{2,1,0:T(4,128)S(1)}, f32[32,48,768]{2,1,0:T(8,128)}) %tuple.64, ...), branch_computations={%region_17.18_spmd, %region_18.19_spmd, %region_19.20_spmd, %regio... | conditional | flops 8429764608 | bytes 28471308 | solution.py:807
  239.7 12.0 %copy.67 = f32[32,48,768]{0,2,1:T(8,128)} copy(f32[32,48,768]{2,1,0:T(8,128)} %get-tuple-element.89) | data formatting | bytes 9437184 | tf_op jit(solution)/shard_map
  252.7 2.0 fusion
  254.8 4.8 %pad.29 = f32[32,96,768]{2,1,0:T(8,128)} pad(f32[32,24,768]{2,1,0:T(8,128)S(1)} %fusion, f32[]{:T(128)} %constant.21.clone), padding=0_0x0_72x0_0 | pad | bytes 11796484 | tf_op jit(solution)/shard_map/cond/branch_1_fun/jit(_pad)/pad | solution.py:805
  268.9 17.5 %shard_map.357.refs_0_ = bf16[4,96,768]{2,1,0:T(8,128)(2,1)} custom-call(bf16[4,96,768]{2,1,0:T(8,128)(2,1)} %pad_maximum_fusion.1.block_ref), custom_call_target="tpu_custom_call" | custom-call | tf_op jit(solution)/shard_map/pallas_call | solution.py:255
  286.4 57.9 %shard_map.358 = bf16[8,4,96,768]{3,2,1,0:T(8,128)(2,1)} custom-call(bf16[4,96,768]{2,1,0:T(8,128)(2,1)} %shard_map.357.refs_0_), custom_call_target="tpu_custom_call" | custom-call | tf_op jit(solution)/shard_map/pallas_call | solution.py:202
  344.3 7.0 %convert_multiply_fusion = f32[8,4,96,768]{3,2,1,0:T(8,128)} fusion(bf16[8,4,96,768]{3,2,1,0:T(8,128)(2,1)} %shard_map.358), kind=kLoop, calls=%fused_computation.11 | loop fusion | flops 4718592 | bytes 14155776 | tf_op jit(solution)/shard_map/mul | solution.py:816
  351.3 11.8 %bitcast_add_fusion = f32[32,96,768]{2,1,0:T(8,128)} fusion(f32[8,4,96,768]{3,2,1,0:T(8,128)} %convert_multiply_fusion, f32[32,96,768]{2,1,0:T(8,128)} %get-tuple-element.139, f32[]{:T(128)S(6)} %min.3), kind=kLoop, calls=%fused_computation.10 | loop fusion | flops 4718592 | bytes 28311556 | tf_op jit(solution)/shard_map/add | solution.py:816
  363.1 27.6 %fusion.12 = (f32[]{:T(128)}, f32[768,768,1]{1,0,2:T(8,128)S(1)}) fusion(f32[32,96,768]{2,1,0:T(8,128)} %bitcast_add_fusion), kind=kOutput, calls=%fused_computation.22 | convolution fusion | flops 21745041408 | bytes 11796484 | tf_op jit(solution)/shard_map/rd,re->de/dot_general | solution.py:617
  391.4 1.7 bitcast_multiply_fusion.gram_ref
  393.1 41.2 %shard_map.359 = f32[768,768]{1,0:T(8,128)} custom-call(f32[768,768]{1,0:T(8,128)} %bitcast_multiply_fusion.gram_ref), custom_call_target="tpu_custom_call" | custom-call | tf_op jit(solution)/shard_map/pallas_call | solution.py:598
  434.3 6.2 %fusion.10.block_ref = f32[4,96,768]{2,1,0:T(8,128)} fusion(f32[768,768]{1,0:T(8,128)} %shard_map.359, f32[32,96,768]{2,1,0:T(8,128)} %bitcast_add_fusion, s32[]{:T(128)S(6)} %select_n.23, f32[]{:T(128)S(6)} %div.13), kind=kOutput, calls=%fused_computation.18 | convolution fusion | flops 2718203904 | bytes 4718600 | tf_op jit(solution)/shard_map/srd,de->sre/dot_general | solution.py:617
  440.6 20.2 %shard_map.360 = f32[4,96,768]{2,1,0:T(8,128)} custom-call(f32[4,96,768]{2,1,0:T(8,128)} %fusion.10.block_ref), custom_call_target="tpu_custom_call" | custom-call | tf_op jit(solution)/shard_map/pallas_call | solution.py:255
  460.8 1.8 fusion.74
  462.6 1.8 fusion.76
  464.4 1.7 fusion.80
  466.1 1.5 fusion.78
  469.1 1.9 fusion.15
  473.0 2.7 fusion.17
  (132 shorter events, 31.3 us)
Async XLA Ops:
  198.9 5.9 %copy-start.1 = (bf16[32,48,768]{2,1,0:T(8,128)(2,1)S(1)}, bf16[32,48,768]{2,1,0:T(8,128)(2,1)}, u32[]{:S(2)}) copy-start(bf16[32,48,768]{2,1,0:T(8,128)(2,1)} %shard_map.356) | copy-start | bytes 7077892
  201.3 2.2 copy-start
  201.3 11.4 %copy-start.28 = (f32[1,768]{1,0:T(1,128)S(1)}, f32[1,768]{1,0:T(1,128)}, u32[]{:S(2)}) copy-start(f32[1,768]{1,0:T(1,128)} %get-tuple-element.81) | copy-start | bytes 9220
  201.3 11.4 %copy-start.31 = (f32[1,768]{1,0:T(1,128)S(1)}, f32[1,768]{1,0:T(1,128)}, u32[]{:S(2)}) copy-start(f32[1,768]{1,0:T(1,128)} %get-tuple-element.82) | copy-start | bytes 9220
  203.6 0.6 copy-start.18
  205.6 2.0 copy-start.21
  205.6 13.4 %copy-start.19 = (bf16[32,1,768]{2,1,0:T(2,128)(2,1)}, bf16[32,1,768]{2,1,0:T(2,128)(2,1)S(1)}, u32[]{:S(2)}) copy-start(bf16[32,1,768]{2,1,0:T(2,128)(2,1)S(1)} %get-tuple-element.122) | copy-start | bytes 147460
  205.6 17.4 %copy-start.22 = (bf16[32,1,768]{2,1,0:T(2,128)(2,1)}, bf16[32,1,768]{2,1,0:T(2,128)(2,1)S(1)}, u32[]{:S(2)}) copy-start(bf16[32,1,768]{2,1,0:T(2,128)(2,1)S(1)} %get-tuple-element.120) | copy-start | bytes 147460
  205.6 16.4 %copy-start.24 = (f32[24,108]{1,0:T(8,128)S(1)}, f32[24,108]{1,0:T(8,128)}, u32[]{:S(2)}) copy-start(f32[24,108]{1,0:T(8,128)} %param.30) | copy-start | bytes 31108
  205.7 16.4 %copy-start.26 = (f32[24,108]{1,0:T(8,128)S(1)}, f32[24,108]{1,0:T(8,128)}, u32[]{:S(2)}) copy-start(f32[24,108]{1,0:T(8,128)} %param.37) | copy-start | bytes 31108
  205.7 16.4 %copy-start.27 = (f32[24,108]{1,0:T(8,128)S(1)}, f32[24,108]{1,0:T(8,128)}, u32[]{:S(2)}) copy-start(f32[24,108]{1,0:T(8,128)} %param.36) | copy-start | bytes 31108
  206.7 0.7 copy-start.12
  206.7 17.5 %copy-start.10 = (bf16[32,4,768]{2,1,0:T(4,128)(2,1)}, bf16[32,4,768]{2,1,0:T(4,128)(2,1)S(1)}, u32[]{:S(2)}) copy-start(bf16[32,4,768]{2,1,0:T(4,128)(2,1)S(1)} %get-tuple-element.126) | copy-start | bytes 589828
  217.0 0.6 copy-start.14
  236.7 31.2 %copy-start.8 = (f32[768,72]{0,1:T(8,128)S(1)}, f32[768,72]{0,1:T(8,128)}, u32[]{:S(2)}) copy-start(f32[768,72]{0,1:T(8,128)} %param.32) | copy-start | bytes 663556
  236.7 31.2 %copy-start.15 = (f32[24,768]{1,0:T(8,128)S(1)}, f32[24,768]{1,0:T(8,128)}, u32[]{:S(2)}) copy-start(f32[24,768]{1,0:T(8,128)} %param.33) | copy-start | bytes 221188
  236.7 31.2 %copy-start.3 = (f32[96,768]{1,0:T(8,128)S(1)}, f32[96,768]{1,0:T(8,128)}, u32[]{:S(2)}) copy-start(f32[96,768]{1,0:T(8,128)} %param.35) | copy-start | bytes 884740
  236.7 31.2 %copy-start.4 = (f32[768,96]{0,1:T(8,128)S(1)}, f32[768,96]{0,1:T(8,128)}, u32[]{:S(2)}) copy-start(f32[768,96]{0,1:T(8,128)} %param.34) | copy-start | bytes 884740
  434.3 26.5 %copy-start.5 = (f32[96,768]{1,0:T(8,128)S(1)}, f32[96,768]{1,0:T(8,128)}, u32[]{:S(2)}) copy-start(f32[96,768]{1,0:T(8,128)} %param.29) | copy-start | bytes 884740
  434.3 28.3 %copy-start.6 = (f32[768,96]{0,1:T(8,128)S(1)}, f32[768,96]{0,1:T(8,128)}, u32[]{:S(2)}) copy-start(f32[768,96]{0,1:T(8,128)} %param.28) | copy-start | bytes 884740
  434.3 30.1 %copy-start.7 = (f32[768,72]{0,1:T(8,128)S(1)}, f32[768,72]{0,1:T(8,128)}, u32[]{:S(2)}) copy-start(f32[768,72]{0,1:T(8,128)} %param.26) | copy-start | bytes 663556
  440.6 25.6 %copy-start.17 = (f32[24,768]{1,0:T(8,128)S(1)}, f32[24,768]{1,0:T(8,128)}, u32[]{:S(2)}) copy-start(f32[24,768]{1,0:T(8,128)} %param.27) | copy-start | bytes 221188
  440.6 27.1 %copy-start.25 = (f32[13,24]{1,0:T(8,128)S(1)}, f32[13,24]{1,0:T(8,128)}, u32[]{:S(2)}) copy-start(f32[13,24]{1,0:T(8,128)} %param.31) | copy-start | bytes 3748
  440.6 27.1 %copy-start.29 = (f32[13,24]{1,0:T(8,128)S(1)}, f32[13,24]{1,0:T(8,128)}, u32[]{:S(2)}) copy-start(f32[13,24]{1,0:T(8,128)} %param.39) | copy-start | bytes 3748
  440.6 27.1 %copy-start.30 = (f32[13,24]{1,0:T(8,128)S(1)}, f32[13,24]{1,0:T(8,128)}, u32[]{:S(2)}) copy-start(f32[13,24]{1,0:T(8,128)} %param.38) | copy-start | bytes 3748
  440.6 28.5 %copy-start.13 = (bf16[32,4,768]{2,1,0:T(4,128)(2,1)S(1)}, bf16[32,4,768]{2,1,0:T(4,128)(2,1)}, u32[]{:S(2)}) copy-start(bf16[32,4,768]{2,1,0:T(4,128)(2,1)} %copy-done.12) | copy-start | bytes 589828
  440.6 30.5 %copy-start.11 = (bf16[32,4,768]{2,1,0:T(4,128)(2,1)S(1)}, bf16[32,4,768]{2,1,0:T(4,128)(2,1)}, u32[]{:S(2)}) copy-start(bf16[32,4,768]{2,1,0:T(4,128)(2,1)} %copy-done.10) | copy-start | bytes 589828
  440.6 30.5 %copy-start.20 = (bf16[32,1,768]{2,1,0:T(2,128)(2,1)S(1)}, bf16[32,1,768]{2,1,0:T(2,128)(2,1)}, u32[]{:S(2)}) copy-start(bf16[32,1,768]{2,1,0:T(2,128)(2,1)} %copy-done.19) | copy-start | bytes 147460
  440.6 31.6 %copy-start.16 = (f32[24,768]{1,0:T(8,128)S(1)}, f32[24,768]{1,0:T(8,128)}, u32[]{:S(2)}) copy-start(f32[24,768]{1,0:T(8,128)} %param.33) | copy-start | bytes 221188
  440.6 32.4 %copy-start.2 = (f32[397,768]{1,0:T(8,128)S(1)}, f32[397,768]{1,0:T(8,128)}, u32[]{:S(2)}) copy-start(f32[397,768]{1,0:T(8,128)} %pad_maximum_fusion) | copy-start | bytes 3658756
  440.6 32.4 %copy-start.9 = (f32[768,72]{0,1:T(8,128)S(1)}, f32[768,72]{0,1:T(8,128)}, u32[]{:S(2)}) copy-start(f32[768,72]{0,1:T(8,128)} %param.32) | copy-start | bytes 663556
  462.6 9.6 %copy-start.23 = (bf16[32,1,768]{2,1,0:T(2,128)(2,1)S(1)}, bf16[32,1,768]{2,1,0:T(2,128)(2,1)}, u32[]{:S(2)}) copy-start(bf16[32,1,768]{2,1,0:T(2,128)(2,1)} %copy-done.22) | copy-start | bytes 147460
